TPU v7x, 256 devices: a whole 4x4x8 slice. The times are simulated.
256 devices in a mesh: dp: 16 (over x_lo, z), mp: 16 (over x_hi, y, core).
Axes of the slice: x: 4 (x_hi: 2, x_lo: 2; x = x_hi * 2 + x_lo), y: 4, z: 8, core: 2. Of those that a mesh axis runs over, the one named last changes fastest.
Arguments:
- stream_left: bfloat16 [2048, 6144], P(None, 'dp'), may hold values from -30 to 30
- stream_right: bfloat16 [2048, 6144], P(None, 'dp'), may hold values from -30 to 30
- scale_left: float32 [6144], P('dp'), may hold values from 0.1 to 1.9
- scale_right: float32 [6144], P('dp'), may hold values from 0.1 to 1.9
- expand_left: bfloat16 [6144, 12288], P('dp', 'mp'), may hold values from -0.078125 to 0.078125
- expand_right: bfloat16 [6144, 12288], P('dp', 'mp'), may hold values from -0.078125 to 0.078125
- shift_left: float32 [12288], P('mp'), may hold values from -3 to 3
- shift_right: float32 [12288], P('mp'), may hold values from -3 to 3
- project_left: bfloat16 [12288, 6144], P('mp', 'dp'), may hold values from -0.0546875 to 0.0546875
- project_right: bfloat16 [12288, 6144], P('mp', 'dp'), may hold values from -0.0546875 to 0.0546875
- offset_left: float32 [6144], P('dp'), may hold values from -3 to 3
- offset_right: float32 [6144], P('dp'), may hold values from -3 to 3
Outputs:
- after_left: bfloat16 [2048, 6144], P('mp', 'dp')
- after_right: bfloat16 [2048, 6144], P('mp', 'dp')
- correlation: float32 [6144, 6144], P('dp', 'mp')
All inputs are finite; a program needn't handle non-finite values.
Results may differ from a plain program's by a relative error of at most 0.014.
Values may be sent and summed in bfloat16 or wider, within the bound.
A program may use at most 64 MiB of HBM per device.

v0:
```python
import jax
import jax.numpy as jnp
from jax import lax
from jax.sharding import PartitionSpec as P

EPS = 1e-06


def layer(streams, scales, expands, shifts, projects, offsets):
    tokens = streams[0].shape[0]
    width = streams[0].shape[1]
    full_width = width * lax.axis_size("dp")
    values = [stream.astype(jnp.float32) for stream in streams]
    local_sums = jnp.stack(
        [jnp.stack([jnp.sum(item, axis=1), jnp.sum(item * item, axis=1)]) for item in values]
    )
    totals = lax.psum(local_sums, "dp")
    which = 0
    mean = totals[which, 0] / full_width
    var = totals[which, 1] / full_width - mean * mean
    scaled = (values[which] - mean[:, None]) * lax.rsqrt(var[:, None] + EPS) * scales[which]
    normed = scaled.astype(jnp.bfloat16)
    pieces = [jnp.dot(normed, expands[0], preferred_element_type=jnp.float32)]
    summed = lax.psum_scatter(
        pieces[0].astype(jnp.bfloat16), "dp", scatter_dimension=0, tiled=True
    ).astype(jnp.float32)
    acts = jax.nn.gelu(summed + shifts[0], approximate=False).astype(jnp.bfloat16)
    pieces = [
        jnp.dot(
            lax.all_gather(acts, "dp", axis=0, tiled=True),
            projects[0],
            preferred_element_type=jnp.float32,
        )
    ]
    partial_out = pieces[0]
    reduced = lax.psum_scatter(
        partial_out.astype(jnp.bfloat16), "mp", scatter_dimension=0, tiled=True
    ).astype(jnp.float32)
    mp_rows = tokens // lax.axis_size("mp")
    first_row = lax.axis_index("mp") * mp_rows
    which = 0
    resid = lax.dynamic_slice_in_dim(values[which], first_row, mp_rows, 0)
    results = [(resid + offsets[which] + reduced).astype(jnp.bfloat16)]
    return results


def per_device(
    stream_left,
    stream_right,
    scale_left,
    scale_right,
    expand_left,
    expand_right,
    shift_left,
    shift_right,
    project_left,
    project_right,
    offset_left,
    offset_right,
):
    after_left = layer(
        [stream_left], [scale_left], [expand_left], [shift_left], [project_left], [offset_left]
    )[0]
    after_right = layer(
        [stream_right],
        [scale_right],
        [expand_right],
        [shift_right],
        [project_right],
        [offset_right],
    )[0]
    total_tokens = after_left.shape[0] * lax.axis_size("mp")
    gathered_right = lax.all_gather(after_right, "dp", axis=1, tiled=True)
    block = lax.psum_scatter(
        lax.dot_general(
            gathered_right, after_left, (((0,), (0,)), ((), ())), preferred_element_type=jnp.float32
        ).astype(jnp.bfloat16),
        "mp",
        scatter_dimension=0,
        tiled=True,
    ).astype(jnp.float32)
    correlation = block.T / total_tokens
    return (after_left, after_right, correlation)


def solution(mesh):
    placed = (
        P(None, "dp"),
        P(None, "dp"),
        P("dp"),
        P("dp"),
        P("dp", "mp"),
        P("dp", "mp"),
        P("mp"),
        P("mp"),
        P("mp", "dp"),
        P("mp", "dp"),
        P("dp"),
        P("dp"),
    )
    return jax.shard_map(
        per_device,
        mesh=mesh,
        in_specs=placed,
        out_specs=(P("mp", "dp"), P("mp", "dp"), P("dp", "mp")),
        check_vma=False,
    )
```

profile of v0, /device:TPU:32, one launch (start us, length us, event | category | flops | bytes accessed | tf_op | source)
XLA Modules:
  0.0 710.8 jit_solution(5102599465901089435)
XLA Ops:
  7.2 2.2 convert_reduce_fusion.1
  9.4 2.0 convert_reduce_fusion
  11.5 62.2 %all-reduce = (f32[1,2,2048]{2,1,0:T(2,128)S(1)}, f32[1,2,2048]{2,1,0:T(2,128)S(1)}) all-reduce(f32[1,2,2048]{2,1,0:T(2,128)S(1)} %maximum_bitcast_fusion, f32[1,2,2048]{2,1,0:T(2,128)S(1)} %maximum_bitcast_fusion.1), channel_id=1, replica_groups=mesh['dp'=16,'mp'=16] {'dp'}, use_global_device_ids=true, to_apply=%region_2.0 | all-reduce | flops 8192 | bytes 65536 | tf_op jit(solution)/shard_map/psum | solution.py:17
  73.8 3.3 convolution_convert_fusion.1
  77.1 0.0 reduce-scatter.6.cloned.1.call-start
  77.2 1.0 copy-done.7
  78.2 4.9 convolution_convert_fusion.2
  83.1 0.0 all-gather.6.cloned.1.call-start
  83.2 69.0 %reduce-scatter.10.cloned.1.call-done = bf16[128,768]{1,0:T(8,128)(2,1)} async-done(((bf16[2048,768]{1,0:T(8,128)(2,1)}), bf16[128,768]{1,0:T(8,128)(2,1)}) %reduce-scatter.10.cloned.1.call-update) | async-done | bytes 196624 | tf_op jit(solution)/shard_map/reduce_scatter | solution.py:24
  152.2 2.5 fusion.11
  154.7 0.0 all-gather.4.cloned.1.call-start
  154.7 74.0 %reduce-scatter.6.cloned.1.call-done = bf16[128,768]{1,0:T(8,128)(2,1)} async-done(((bf16[2048,768]{1,0:T(8,128)(2,1)}), bf16[128,768]{1,0:T(8,128)(2,1)}) %reduce-scatter.6.cloned.1.call-update) | async-done | bytes 196624 | tf_op jit(solution)/shard_map/reduce_scatter | solution.py:24
  228.7 2.5 fusion.8
  231.2 0.0 reduce-scatter.12.cloned.1.call-start
  231.3 72.1 %all-gather.6.cloned.1.call-done = bf16[2048,768]{1,0:T(8,128)(2,1)} async-done(((bf16[128,768]{1,0:T(8,128)(2,1)}), bf16[2048,768]{1,0:T(8,128)(2,1)}) %all-gather.6.cloned.1.call-update) | async-done | bytes 3145744 | tf_op jit(solution)/shard_map/all_gather | solution.py:30
  303.4 4.9 convolution_convert_fusion.3
  308.2 0.0 reduce-scatter.8.cloned.1.call-start
  308.3 69.5 %all-gather.4.cloned.1.call-done = bf16[2048,768]{1,0:T(8,128)(2,1)} async-done(((bf16[128,768]{1,0:T(8,128)(2,1)}), bf16[2048,768]{1,0:T(8,128)(2,1)}) %all-gather.4.cloned.1.call-update) | async-done | bytes 3145744 | tf_op jit(solution)/shard_map/all_gather | solution.py:30
  377.8 4.8 convolution_convert_fusion.4
  382.7 0.0 all-gather.8.cloned.1.call-start
  382.8 1.8 convert_element_type.62
  384.6 72.2 %reduce-scatter.12.cloned.1.call-done = bf16[128,384]{1,0:T(8,128)(2,1)} async-done(((bf16[2048,384]{1,0:T(8,128)(2,1)}), bf16[128,384]{1,0:T(8,128)(2,1)}) %reduce-scatter.12.cloned.1.call-update) | async-done | bytes 98320 | tf_op jit(solution)/shard_map/reduce_scatter | solution.py:36
  456.8 1.6 add_convert_fusion
  458.5 0.0 reduce-scatter.14.cloned.1.call-start
  458.6 3.2 convert_element_type.54
  461.8 75.3 %reduce-scatter.8.cloned.1.call-done = bf16[128,384]{1,0:T(8,128)(2,1)} async-done(((bf16[2048,384]{1,0:T(8,128)(2,1)}), bf16[128,384]{1,0:T(8,128)(2,1)}) %reduce-scatter.8.cloned.1.call-update) | async-done | bytes 98320 | tf_op jit(solution)/shard_map/reduce_scatter | solution.py:36
  537.1 1.0 add_convert_fusion.1
  538.1 69.9 %all-gather.8.cloned.1.call-done = bf16[128,6144]{1,0:T(8,128)(2,1)} async-done(((bf16[128,384]{1,0:T(8,128)(2,1)}), bf16[128,6144]{1,0:T(8,128)(2,1)}) %all-gather.8.cloned.1.call-update) | async-done | bytes 1572880 | tf_op jit(solution)/shard_map/all_gather | solution.py:73
  608.0 5.0 convolution_convert_fusion
  613.0 89.0 %reduce-scatter.14.cloned.1.call-done = bf16[384,384]{1,0:T(8,128)(2,1)} async-done(((bf16[6144,384]{1,0:T(8,128)(2,1)}), bf16[384,384]{1,0:T(8,128)(2,1)}) %reduce-scatter.14.cloned.1.call-update) | async-done | bytes 294928 | tf_op jit(solution)/shard_map/reduce_scatter | solution.py:74
  701.9 1.0 multiply_bitcast_fusion
  703.0 1.1 copy.15
  (37 shorter events, 0.3 us)
Async XLA Ops:
  7.2 66.6 %copy-start = (bf16[384,768]{1,0:T(8,128)(2,1)S(1)}, bf16[384,768]{1,0:T(8,128)(2,1)}, u32[]{:S(2)}) copy-start(bf16[384,768]{1,0:T(8,128)(2,1)} %param.17) | copy-start | bytes 1769476
  7.2 66.6 %copy-start.1 = (bf16[2048,384]{1,0:T(8,128)(2,1)S(1)}, bf16[2048,384]{1,0:T(8,128)(2,1)}, u32[]{:S(2)}) copy-start(bf16[2048,384]{1,0:T(8,128)(2,1)} %param.13) | copy-start | bytes 4718596
  7.2 66.6 %copy-start.10 = (f32[384]{0:T(512)S(1)}, f32[384]{0:T(512)}, u32[]{:S(2)}) copy-start(f32[384]{0:T(512)} %param.15) | copy-start | bytes 4612
  7.2 145.0 %reduce-scatter.10.cloned.1.call-start = ((), (), s32[]{:S(2)}) async-start(), calls=%async_computation.8 | async-start | bytes 3342336 | tf_op jit(solution)/shard_map/reduce_scatter | solution.py:24
  77.1 1.1 copy-start.7
  77.1 1.1 copy-start.11
  77.1 151.6 %reduce-scatter.6.cloned.1.call-start = ((), (), s32[]{:S(2)}) async-start(), calls=%async_computation.5 | async-start | bytes 3342336 | tf_op jit(solution)/shard_map/reduce_scatter | solution.py:24
  83.1 69.1 %copy-start.3 = (f32[768]{0:T(1024)S(1)}, f32[768]{0:T(1024)}, u32[]{:S(2)}) copy-start(f32[768]{0:T(1024)} %param.19) | copy-start | bytes 9220
  83.1 145.6 %copy-start.4 = (f32[768]{0:T(1024)S(1)}, f32[768]{0:T(1024)}, u32[]{:S(2)}) copy-start(f32[768]{0:T(1024)} %param.18) | copy-start | bytes 9220
  83.1 220.3 %copy-start.8 = (bf16[768,384]{1,0:T(8,128)(2,1)S(1)}, bf16[768,384]{1,0:T(8,128)(2,1)}, u32[]{:S(2)}) copy-start(bf16[768,384]{1,0:T(8,128)(2,1)} %param.21) | copy-start | bytes 1769476
  83.1 220.2 %all-gather.6.cloned.1.call-start = ((), (), s32[]{:S(2)}) async-start(), calls=%async_computation.9 | async-start | bytes 3342336 | tf_op jit(solution)/shard_map/all_gather | solution.py:30
  154.7 223.1 %all-gather.4.cloned.1.call-start = ((), (), s32[]{:S(2)}) async-start(), calls=%async_computation.6 | async-start | bytes 3342336 | tf_op jit(solution)/shard_map/all_gather | solution.py:30
  231.2 146.6 %copy-start.9 = (bf16[768,384]{1,0:T(8,128)(2,1)S(1)}, bf16[768,384]{1,0:T(8,128)(2,1)}, u32[]{:S(2)}) copy-start(bf16[768,384]{1,0:T(8,128)(2,1)} %param.20) | copy-start | bytes 1769476
  231.2 225.6 %reduce-scatter.12.cloned.1.call-start = ((), (), s32[]{:S(2)}) async-start(), calls=%async_computation.10 | async-start | bytes 1671168 | tf_op jit(solution)/shard_map/reduce_scatter | solution.py:36
  308.2 228.8 %reduce-scatter.8.cloned.1.call-start = ((), (), s32[]{:S(2)}) async-start(), calls=%async_computation.7 | async-start | bytes 1671168 | tf_op jit(solution)/shard_map/reduce_scatter | solution.py:36
  382.7 74.1 %copy-start.5 = (f32[384]{0:T(512)S(1)}, f32[384]{0:T(512)}, u32[]{:S(2)}) copy-start(f32[384]{0:T(512)} %param.23) | copy-start | bytes 4612
  382.7 225.3 %all-gather.8.cloned.1.call-start = ((), (), s32[]{:S(2)}) async-start(), calls=%async_computation.11 | async-start | bytes 1671168 | tf_op jit(solution)/shard_map/all_gather | solution.py:73
  384.6 152.5 %copy-start.6 = (f32[384]{0:T(512)S(1)}, f32[384]{0:T(512)}, u32[]{:S(2)}) copy-start(f32[384]{0:T(512)} %param.22) | copy-start | bytes 4612
  458.5 243.4 %reduce-scatter.14.cloned.1.call-start = ((), (), s32[]{:S(2)}) async-start(), calls=%async_computation.12 | async-start | bytes 5013504 | tf_op jit(solution)/shard_map/reduce_scatter | solution.py:74
  538.1 74.9 %copy-start.2 = (bf16[128,384]{1,0:T(8,128)(2,1)}, bf16[128,384]{1,0:T(8,128)(2,1)S(1)}, u32[]{:S(2)}) copy-start(bf16[128,384]{1,0:T(8,128)(2,1)S(1)} %add_convert_fusion.1) | copy-start | bytes 294916
Sparse Core Ops, SparseCore 0:
  77.3 74.8 reduce-scatter.9
  154.7 73.9 reduce-scatter.5
  230.5 72.8 all-gather.5
  305.6 72.2 all-gather.3
  381.9 74.8 reduce-scatter.11
  461.5 75.5 reduce-scatter.7
  539.5 68.4 all-gather.7
  613.1 88.7 reduce-scatter.13
where the time goes:
time: 711 us
  waiting for transfers between devices  591 us (83%)
  blocking collectives  62.2 us (9%)
  matrix products  22.9 us (3%)
  other arithmetic  18 us (3%)
  between operations  14.3 us (2%)
    reduce_scatter x2, waiting for transfers between devices, layer(): lax.psum_scatter(partial_out.astype(jnp.bfloat16), 'mp', scatter_dimensio...  148 us
    reduce_scatter x2, waiting for transfers between devices, layer(): lax.psum_scatter(pieces[0].astype(jnp.bfloat16), 'dp', scatter_dimension=...  143 us
    all_gather x2, waiting for transfers between devices, layer(): lax.all_gather(acts, 'dp', axis=0, tiled=True)  142 us
    reduce_scatter x1, waiting for transfers between devices, per_device(): lax.psum_scatter(lax.dot_general(gathered_right, after_left, (((0,), (0,)...  89 us
    all_gather x1, waiting for transfers between devices, per_device(): gathered_right = lax.all_gather(after_right, 'dp', axis=1, tiled=True)  69.9 us
    psum x1, blocking collectives, layer(): totals = lax.psum(local_sums, 'dp')  62.2 us
  transfers between devices with their start and end apart: 8, of which 8 were waited for; matrix products, arithmetic and copies ran while one was open for 4% of the time, Pallas kernels for 0%

commit v1 on v0

v1 whole, which is shorter than its diff:
```python
import functools

import jax
import jax.numpy as jnp
from jax import lax
from jax.experimental import pallas as pl
from jax.experimental.pallas import tpu as pltpu
from jax.sharding import PartitionSpec as P

EPS = 1e-06
F32 = jnp.float32
BF16 = jnp.bfloat16
MESH = pl.DeviceIdType.MESH

NZ, NY = 8, 4
TOK = 128
W = 384
HID = 768


class Slots:
    def __init__(self):
        self.count = 0

    def take(self, n):
        first = self.count
        self.count += n
        return first


SLOTS = Slots()
S_STAT1 = SLOTS.take(16)
S_STAT2 = SLOTS.take(16)
S_EXP = [SLOTS.take(1) for _ in range(2)]
S_PROJ = [SLOTS.take(1) for _ in range(2)]
S_GAIN = [SLOTS.take(1) for _ in range(2)]
S_STREAM = [SLOTS.take(2) for _ in range(2)]
S_RS = [SLOTS.take(14) for _ in range(2)]
S_AG = [SLOTS.take(8) for _ in range(2)]
S_CORE = [SLOTS.take(1) for _ in range(2)]
S_Y = [SLOTS.take(4) for _ in range(2)]
S_X = [SLOTS.take(3) for _ in range(2)]
S_LEFT = SLOTS.take(8)
S_LEFTC = SLOTS.take(8)
S_TURN = SLOTS.take(1)
S_PAIR = SLOTS.take(1)
S_RIGHT = SLOTS.take(8)
N_SEMS = SLOTS.count


def spread(row, size=TOK):
    return jnp.broadcast_to(row, (size, size)).T


def kernel(
    s_l, s_r, g_l, g_r, e_l, e_r, b_l, b_r, p_l, p_r, o_l, o_r,
    a_l, a_r, corr,
    st1, st2, r1, r2, xe, xp, xg, xs, nrm, rr, rsb, act, yb, cr, ys, yr, xt, xr, al, at,
    ssem, rsem,
):
    streams, gains, expands, shifts = (s_l, s_r), (g_l, g_r), (e_l, e_r), (b_l, b_r)
    projects, offsets, afters = (p_l, p_r), (o_l, o_r), (a_l, a_r)
    i, j = lax.axis_index("dp"), lax.axis_index("mp")
    xl, z = lax.div(i, 8), lax.rem(i, 8)
    xh, y, c = lax.div(j, 8), lax.rem(lax.div(j, 2), 4), lax.rem(j, 2)

    def dev(xl_, z_, xh_, y_, c_):
        return (xl_ * 8 + z_, xh_ * 8 + y_ * 2 + c_)

    def copy(src, dst, sem, to, rsem_at=None):
        return pltpu.make_async_remote_copy(
            src_ref=src,
            dst_ref=dst,
            send_sem=ssem.at[sem],
            recv_sem=rsem.at[sem if rsem_at is None else rsem_at],
            device_id=to,
            device_id_type=MESH,
        )

    x_peer = dev(1 - xl, z, xh, y, c)
    w_peer = dev(1 - xl, z, 1 - xh, y, c)
    c_peer = dev(xl, z, xh, y, 1 - c)
    z_next = dev(xl, lax.rem(z + 1, 8), xh, y, c)
    z_prev = dev(xl, lax.rem(z + 7, 8), xh, y, c)

    barrier = pltpu.get_barrier_semaphore()

    def greet(d, _):
        pl.semaphore_signal(barrier, inc=1, device_id=(lax.rem(i + d, 16), j), device_id_type=MESH)
        pl.semaphore_signal(barrier, inc=1, device_id=(i, lax.rem(j + d, 16)), device_id_type=MESH)
        return 0

    lax.fori_loop(1, 16, greet, 0)
    pl.semaphore_signal(barrier, inc=1, device_id=w_peer, device_id_type=MESH)

    @pl.when(i != j)
    def _():
        pl.semaphore_signal(barrier, inc=1, device_id=(j, i), device_id_type=MESH)
        pl.semaphore_wait(barrier, 32)

    @pl.when(i == j)
    def _():
        pl.semaphore_wait(barrier, 31)

    sent = []

    def start(cp):
        cp.start()
        sent.append(cp)
        return cp

    def stream_copy(k):
        rows = pl.multiple_of((1 - xl) * 1024 + c * 512, 512)
        return copy(
            streams[k].at[pl.ds(rows, 512)],
            xs.at[k, pl.ds(pl.multiple_of(c * 512, 512), 512)],
            S_STREAM[k],
            w_peer,
        )

    def stream_forward(k):
        part = xs.at[k, pl.ds(pl.multiple_of(c * 512, 512), 512)]
        return copy(part, part, S_STREAM[k] + 1, c_peer)

    str_cp = [stream_copy(k) for k in range(2)]
    exp_cp = [copy(expands[k], xe.at[k], S_EXP[k], x_peer) for k in range(2)]
    prj_cp = [copy(projects[k], xp.at[k], S_PROJ[k], x_peer) for k in range(2)]
    gain_cp = [copy(gains[k], xg.at[k], S_GAIN[k], x_peer) for k in range(2)]
    start(gain_cp[0])
    start(gain_cp[1])
    start(str_cp[0])
    start(exp_cp[0])

    mine = pl.ds(pl.multiple_of(j * TOK, TOK), TOK)
    st1[...] = jnp.zeros((8, TOK), F32)
    for k in range(2):
        v = streams[k][mine, :].astype(F32)
        for n, col in enumerate((v, v * v)):
            total = jnp.sum(col, axis=1, keepdims=True)
            st1[2 * k + n : 2 * k + n + 1, :] = jnp.broadcast_to(total, (TOK, TOK)).T[0:1, :]
    r1[0] = st1[...]

    def stat1(d):
        return copy(st1, r1.at[d], S_STAT1 + d, (lax.rem(i + d, 16), j))

    def stat2(d):
        return copy(st2, r2.at[j], S_STAT2 + d, (i, lax.rem(j + d, 16)))

    def run(fn, lo=1, hi=16):
        def body(d, _):
            fn(d)
            return 0

        lax.fori_loop(lo, hi, body, 0)

    run(lambda d: stat1(d).start())
    run(lambda d: stat1(d).wait_recv())
    totals = r1[0]
    for d in range(1, 16):
        totals = totals + r1[d]
    totals = totals * (1.0 / 6144.0)
    st2[...] = jnp.zeros((8, TOK), F32)
    for k in range(2):
        mean = totals[2 * k : 2 * k + 1, :]
        var = totals[2 * k + 1 : 2 * k + 2, :] - mean * mean
        st2[2 * k : 2 * k + 1, :] = mean
        st2[2 * k + 1 : 2 * k + 2, :] = lax.rsqrt(var + EPS)
    r2[j] = st2[...]
    run(lambda d: stat2(d).start())
    run(lambda d: stat2(d).wait_recv())

    def normalise(k, part, r):
        t = xl * 8 + r
        stats = r2[t]
        mean = spread(stats[2 * k : 2 * k + 1, :])
        rstd = spread(stats[2 * k + 1 : 2 * k + 2, :])
        if part == 0:
            v = streams[k][pl.ds(pl.multiple_of(t * TOK, TOK), TOK), :]
            gain = gains[k][...]
        else:
            v = xs[k, pl.ds(pl.multiple_of(r * TOK, TOK), TOK), :]
            gain = xg[k]
        mean, rstd = (jnp.concatenate([q, q, q], axis=1) for q in (mean, rstd))
        nrm[k, r, part] = ((v.astype(F32) - mean) * rstd * gain).astype(BF16)

    def stream_in(k):
        str_cp[k].wait_recv()
        start(stream_forward(k))

    gain_cp[0].wait_recv()
    gain_cp[1].wait_recv()
    run(lambda r: normalise(0, 0, r), 0, 8)
    stream_in(0)
    start(str_cp[1])
    stream_forward(0).wait_recv()
    run(lambda r: normalise(0, 1, r), 0, 8)
    exp_cp[0].wait_recv()
    start(exp_cp[1])

    def cols(h):
        return slice(h * W, (h + 1) * W)

    def partial_pre(k, r, h):
        own = jnp.dot(nrm[k, r, 0], expands[k][:, cols(h)], preferred_element_type=F32)
        return own + jnp.dot(nrm[k, r, 1], xe[k, :, cols(h)], preferred_element_type=F32)

    def rs_copy(k, s, h):
        return copy(rsb.at[k, s, h], rr.at[k, s, h], S_RS[k] + 2 * s + h, (z_next, z_prev)[h])

    def rs_step(k, s, first=False):
        for h in range(2):
            r = lax.rem(z + 7 - s + 8, 8) if h == 0 else lax.rem(z + 1 + s, 8)
            acc = partial_pre(k, r, h)
            if not first:
                rs_copy(k, s - 1, h).wait_recv()
                acc = acc + rr[k, s - 1, h].astype(F32)
            rsb[k, s, h] = acc.astype(BF16)
            rs_copy(k, s, h).start()

    def rs_finish(k):
        for h in range(2):
            acc = partial_pre(k, z, h) + shifts[k][:, cols(h)]
            rs_copy(k, 6, h).wait_recv()
            acc = acc + rr[k, 6, h].astype(F32)
            act[k, z, h] = (0.5 * acc * (1.0 + lax.erf(acc * (0.5 ** 0.5)))).astype(BF16)

    def ag_copy(k, s, way):
        if way == 0:
            r, to = lax.rem(z - s + 8, 8), z_next
        else:
            r, to = lax.rem(z + s, 8), z_prev
        ref = act.at[k, r, way] if isinstance(s, int) and s == 3 else act.at[k, r]
        return copy(ref, ref, S_AG[k] + 2 * s + way, to)

    def ag_step(k, s, first=False):
        for way in range(2):
            if not first:
                ag_copy(k, s - 1, way).wait_recv()
            ag_copy(k, s, way).start()

    def ag_finish(k):
        for way in range(2):
            ag_copy(k, 3, way).wait_recv()

    def gemm2(k, r):
        for b, weight in enumerate((projects[k], xp.at[k])):
            out = jnp.dot(act[k, r, 0], weight[0:W, :], preferred_element_type=F32)
            out = out + jnp.dot(act[k, r, 1], weight[W:HID, :], preferred_element_type=F32)
            yb[k, lax.rem(r, 2), lax.div(r, 2), b] = out.astype(BF16)

    def core_copy(k):
        return copy(yb.at[k, 1 - c], cr.at[k], S_CORE[k], c_peer)

    def y_copy(k, d):
        return copy(ys.at[k, d - 1], yr.at[k, d - 1], S_Y[k] + d, dev(xl, z, xh, lax.rem(y + d, 4), c))

    def chip_sum(k, t):
        return yb[k, c, t].astype(F32) + cr[k, t].astype(F32)

    def y_start(k):
        core_copy(k).wait_recv()
        for d in (2, 1, 3):
            ys[k, d - 1] = chip_sum(k, lax.rem(y + d, 4)).astype(BF16)
            start(y_copy(k, d))

    def x_copy_a(k):
        return copy(
            xt.at[k, 1], xr.at[k, xh], S_X[k], dev(1 - xl, z, xl, y, c), S_X[k] + xh
        )

    def x_copy_a_in(k, n):
        return copy(xt.at[k, 1], xr.at[k, n], S_X[k], x_peer, S_X[k] + n)

    def x_copy_b(k):
        return copy(xt.at[k, 0], xr.at[k, 2], S_X[k] + 2, dev(xl, z, 1 - xh, y, c))

    def x_start(k):
        total = chip_sum(k, y)
        for d in (1, 3, 2):
            y_copy(k, d).wait_recv()
            total = total + yr[k, d - 1].astype(F32)
        xt[k] = total.astype(BF16)
        start(x_copy_a(k))

        @pl.when(xh != xl)
        def _():
            x_copy_b(k).start()

    def finish(k):
        def put(branch):
            resid = streams[k][mine, :].astype(F32) + offsets[k][...]
            afters[k][...] = (resid + branch).astype(BF16)

        @pl.when(xh != xl)
        def _():
            x_copy_a_in(k, 0).wait_recv()
            x_copy_a_in(k, 1).wait_recv()
            put(xr[k, 0].astype(F32) + xr[k, 1].astype(F32))
            x_copy_b(k).wait_send()

        @pl.when(xh == xl)
        def _():
            x_copy_b(k).wait_recv()
            put(xt[k, 0].astype(F32) + xr[k, 2].astype(F32))

    rs_step(0, 0, True)
    run(lambda s: rs_step(0, s), 1, 7)
    stream_in(1)
    exp_cp[1].wait_recv()
    start(prj_cp[0])
    start(prj_cp[1])
    run(lambda r: normalise(1, 0, r), 0, 8)
    stream_forward(1).wait_recv()
    run(lambda r: normalise(1, 1, r), 0, 8)
    rs_finish(0)

    ag_step(0, 0, True)
    rs_step(1, 0, True)

    def both(q, _):
        rs_step(1, 2 * q + 1)
        ag_step(0, q + 1)
        rs_step(1, 2 * q + 2)
        return 0

    lax.fori_loop(0, 2, both, 0)
    ag_step(0, 3)
    run(lambda s: rs_step(1, s), 5, 7)
    rs_finish(1)

    ag_step(1, 0, True)
    ag_finish(0)
    prj_cp[0].wait_recv()
    run(lambda r: gemm2(0, r), 0, 8)
    start(core_copy(0))
    ag_step(1, 1)
    y_start(0)
    ag_step(1, 2)
    x_start(0)
    ag_step(1, 3)
    finish(0)

    q = xh * 4 + y
    al[j] = a_l[...]

    def left_copy(d):
        to = lax.rem(q + d, 8)
        return copy(a_l, al.at[j], S_LEFT + d, (i, to * 2 + c))

    def left_forward(d):
        ref = al.at[lax.rem(q - d + 8, 8) * 2 + c]
        return copy(ref, ref, S_LEFTC + d, c_peer)

    run(lambda d: left_copy(d).start(), 1, 8)
    left_forward(0).start()
    ag_finish(1)
    prj_cp[1].wait_recv()
    run(lambda r: gemm2(1, r), 0, 8)
    start(core_copy(1))
    y_start(1)

    def left_pass(d):
        left_copy(d).wait_recv()
        left_forward(d).start()

    run(left_pass, 1, 8)
    x_start(1)
    finish(1)

    here = at.at[z, xl]
    turn = copy(a_r, at.at[lax.rem(j, 8), lax.div(j, 8)], S_TURN, (j, i))

    @pl.when(i != j)
    def _():
        turn.start()
        turn.wait()

    @pl.when(i == j)
    def _():
        at[z, xl] = a_r[...]

    pair = start(copy(here, here, S_PAIR, x_peer))
    pair.wait_recv()

    def right_copy(s, way):
        if way == 0:
            r, to = lax.rem(z - s + 8, 8), z_next
        else:
            r, to = lax.rem(z + s, 8), z_prev
        ref = at.at[r, way] if s == 3 else at.at[r]
        return copy(ref, ref, S_RIGHT + 2 * s + way, to)

    def add(r, first=False):
        total = None
        for n in range(2):
            term = lax.dot_general(
                al[n * 8 + r], at[r, n], (((0,), (0,)), ((), ())), preferred_element_type=F32
            )
            total = term if total is None else total + term
        corr[...] = total if first else corr[...] + total

    for way in range(2):
        start(right_copy(0, way))
    run(lambda d: left_forward(d).wait_recv(), 0, 8)
    add(z, True)
    for s in range(1, 4):
        for way in range(2):
            right_copy(s - 1, way).wait_recv()
            start(right_copy(s, way))
        add(lax.rem(z - s + 8, 8))
        add(lax.rem(z + s, 8))
    for way in range(2):
        right_copy(3, way).wait_recv()
    add(lax.rem(z + 4, 8))
    corr[...] = corr[...] * (1.0 / 2048.0)

    for cp in sent:
        cp.wait_send()
    run(lambda d: stat1(d).wait_send())
    run(lambda d: stat2(d).wait_send())
    for k in range(2):
        for h in range(2):
            run(lambda s: rs_copy(k, s, h).wait_send(), 0, 7)
            for s in range(4):
                ag_copy(k, s, h).wait_send()
    run(lambda d: left_copy(d).wait_send(), 1, 8)
    run(lambda d: left_forward(d).wait_send(), 0, 8)


def per_device(s_l, s_r, g_l, g_r, e_l, e_r, b_l, b_r, p_l, p_r, o_l, o_r):
    row = lambda v: v.reshape(1, -1)
    vm = pl.BlockSpec(memory_space=pltpu.VMEM)
    tile = (TOK, W)
    return pl.pallas_call(
        kernel,
        out_shape=(
            jax.ShapeDtypeStruct(tile, BF16),
            jax.ShapeDtypeStruct(tile, BF16),
            jax.ShapeDtypeStruct((W, W), F32),
        ),
        in_specs=[vm] * 12,
        out_specs=(vm, vm, vm),
        scratch_shapes=[
            pltpu.VMEM((8, TOK), F32),
            pltpu.VMEM((8, TOK), F32),
            pltpu.VMEM((16, 8, TOK), F32),
            pltpu.VMEM((16, 8, TOK), F32),
            pltpu.VMEM((2, W, HID), BF16),
            pltpu.VMEM((2, HID, W), BF16),
            pltpu.VMEM((2, 1, W), F32),
            pltpu.VMEM((2, 1024, W), BF16),
            pltpu.VMEM((2, 8, 2) + tile, BF16),
            pltpu.VMEM((2, 7, 2) + tile, BF16),
            pltpu.VMEM((2, 7, 2) + tile, BF16),
            pltpu.VMEM((2, 8, 2) + tile, BF16),
            pltpu.VMEM((2, 2, 4, 2) + tile, BF16),
            pltpu.VMEM((2, 4, 2) + tile, BF16),
            pltpu.VMEM((2, 3, 2) + tile, BF16),
            pltpu.VMEM((2, 3, 2) + tile, BF16),
            pltpu.VMEM((2, 2) + tile, BF16),
            pltpu.VMEM((2, 3) + tile, BF16),
            pltpu.VMEM((16,) + tile, BF16),
            pltpu.VMEM((8, 2) + tile, BF16),
            pltpu.SemaphoreType.DMA((N_SEMS,)),
            pltpu.SemaphoreType.DMA((N_SEMS,)),
        ],
        compiler_params=pltpu.CompilerParams(
            collective_id=0, has_side_effects=True, vmem_limit_bytes=56 * 1024 * 1024
        ),
    )(s_l, s_r, row(g_l), row(g_r), e_l, e_r, row(b_l), row(b_r), p_l, p_r, row(o_l), row(o_r))


def solution(mesh):
    placed = (
        P(None, "dp"),
        P(None, "dp"),
        P("dp"),
        P("dp"),
        P("dp", "mp"),
        P("dp", "mp"),
        P("mp"),
        P("mp"),
        P("mp", "dp"),
        P("mp", "dp"),
        P("dp"),
        P("dp"),
    )
    return jax.shard_map(
        per_device,
        mesh=mesh,
        in_specs=placed,
        out_specs=(P("mp", "dp"), P("mp", "dp"), P("dp", "mp")),
        check_vma=False,
    )
```

time: 711 us -> 204 us (0.29)
  waiting for transfers between devices: 591 us -> 0 us
  Pallas kernels: 0 us -> 187 us
  blocking collectives: 62.2 us -> 0 us
  matrix products: 22.9 us -> 0 us
  other arithmetic: 18 us -> 0 us
  between operations: 14.3 us -> 0.64 us
  local copies, waits for them, and re-layouts: 2.08 us -> 12.6 us
    reduce_scatter x5 -> x0, waiting for transfers between devices: 379 us -> none  [the longest x2 148 us: layer(): lax.psum_scatter(partial_out.astype(jnp.bfloat16), 'mp', scatter_dimensio...]
    all_gather x3 -> x0, waiting for transfers between devices: 212 us -> none  [the longest x2 142 us: layer(): lax.all_gather(acts, 'dp', axis=0, tiled=True)]
    pallas_call x0 -> x1, Pallas kernels: none -> 187 us  [per_device(): pl.pallas_call(kernel, out_shape=(jax.ShapeDtypeStruct(tile, BF16), jax.S...]
    psum x1 -> x0, blocking collectives: 62.2 us -> none  [layer(): totals = lax.psum(local_sums, 'dp')]
    dot_general x5 -> x0, matrix products: 22.9 us -> none  [the longest x2 9.7 us: layer(): jnp.dot(lax.all_gather(acts, 'dp', axis=0, tiled=True), projects[0], pref...]
    convert_element_type x6 -> x0, other arithmetic: 12.7 us -> none  [the longest x2 5.08 us: layer(): values = [stream.astype(jnp.float32) for stream in streams]]
    reshape x0 -> x6, local copies, waits for them, and re-layouts: none -> 7.55 us  [per_device(): row = lambda v: v.reshape(1, -1)]
  transfers between devices with their start and end apart: 8 -> 0, of which waited for: 8 -> 0; matrix products, arithmetic and copies ran while one was open for 4% -> 0% of each run, Pallas kernels for 0% -> 0%
where the time goes in v1:
time: 204 us; the launch traced here: 200 us
  Pallas kernels  187 us (92%)
  local copies, waits for them, and re-layouts  12.6 us (6%)
    pallas_call x1, Pallas kernels, per_device(): pl.pallas_call(kernel, out_shape=(jax.ShapeDtypeStruct(tile, BF16), jax.S...  187 us
    reshape x6, local copies, waits for them, and re-layouts, per_device(): row = lambda v: v.reshape(1, -1)  7.55 us
    unnamed x3, local copies, waits for them, and re-layouts  5 us

profile of v1, /device:TPU:32, one launch (start us, length us, event | category | flops | bytes accessed | tf_op | source)
XLA Modules:
  0.0 199.9 jit_solution(4402476657736199108)
XLA Ops:
  0.6 1.2 reshape.24.g_l
  1.9 1.3 reshape.25.g_r
  3.1 1.2 reshape.28.o_l
  4.4 1.3 reshape.29.o_r
  5.7 1.3 reshape.26.b_l
  6.9 1.3 reshape.27.b_r
  8.2 186.7 %shard_map.139 = (bf16[128,384]{1,0:T(8,128)(2,1)}, bf16[128,384]{1,0:T(8,128)(2,1)}, f32[384,384]{1,0:T(8,128)}) custom-call(bf16[2048,384]{1,0:T(8,128)(2,1)} %s_l.1, bf16[2048,384]{1,0:T(8,128)(2,1)} %s_r.1, f32[1,384]{1,0:T(1,128)} %reshape.24.g_l, f32[1,384]{1,0:T(1,128)} %reshape.25.g_r, bf16[384,768]{1,0:T(8,128)(2,1)} %e_l.1, bf16[384,768]{1,0:T(8,128)(2,1)} %e_r.1, ...), custom_call_target="tpu_custom_call" | custom-call | tf_op jit(solution)/shard_map/pallas_call | solution.py:434
  194.9 1.5 copy.18
  196.5 1.5 copy.19
  198.0 1.9 copy.20

commit v2 on v1

v2 whole, which is shorter than its diff:
```python
import functools

import jax
import jax.numpy as jnp
from jax import lax
from jax.experimental import pallas as pl
from jax.experimental.pallas import tpu as pltpu
from jax.sharding import PartitionSpec as P

EPS = 1e-06
F32 = jnp.float32
BF16 = jnp.bfloat16
MESH = pl.DeviceIdType.MESH

NZ, NY = 8, 4
TOK = 128
W = 384
HID = 768


class Slots:
    def __init__(self):
        self.count = 0

    def take(self, n):
        first = self.count
        self.count += n
        return first


SLOTS = Slots()
S_STAT1 = SLOTS.take(16)
S_STAT2 = SLOTS.take(16)
S_EXP = [SLOTS.take(1) for _ in range(2)]
S_PROJ = [SLOTS.take(1) for _ in range(2)]
S_GAIN = [SLOTS.take(1) for _ in range(2)]
S_STREAM = [SLOTS.take(2) for _ in range(2)]
S_RS = [SLOTS.take(28) for _ in range(2)]
S_AG = [SLOTS.take(16) for _ in range(2)]
S_CORE = [SLOTS.take(1) for _ in range(2)]
S_Y = [SLOTS.take(4) for _ in range(2)]
S_X = [SLOTS.take(3) for _ in range(2)]
S_LEFT = SLOTS.take(8)
S_LEFTC = SLOTS.take(8)
S_TURN = SLOTS.take(1)
S_PAIR = SLOTS.take(1)
S_RIGHT = SLOTS.take(16)
N_SEMS = SLOTS.count


def spread(row, size=TOK):
    return jnp.broadcast_to(row, (size, size)).T


def kernel(
    s_l, s_r, g_l, g_r, e_l, e_r, b_l, b_r, p_l, p_r, o_l, o_r,
    a_l, a_r, corr,
    st1, st2, r1, r2, xe, xp, xg0, xg1, xs, nrm, rr, rsb, act, yb, cr, ys, yr, xt, xr, al, at,
    sc, sv, ev, pv, ssem, rsem, lsem,
):
    streams, gains, expands, shifts = (s_l, s_r), (g_l, g_r), (e_l, e_r), (b_l, b_r)
    projects, offsets, afters, xg = (p_l, p_r), (o_l, o_r), (a_l, a_r), (xg0, xg1)
    i, j = lax.axis_index("dp"), lax.axis_index("mp")
    xl, z = lax.div(i, 8), lax.rem(i, 8)
    xh, y, c = lax.div(j, 8), lax.rem(lax.div(j, 2), 4), lax.rem(j, 2)

    def dev(xl_, z_, xh_, y_, c_):
        return (xl_ * 8 + z_, xh_ * 8 + y_ * 2 + c_)

    def copy(src, dst, sem, to, rsem_at=None):
        return pltpu.make_async_remote_copy(
            src_ref=src,
            dst_ref=dst,
            send_sem=ssem.at[sem],
            recv_sem=rsem.at[sem if rsem_at is None else rsem_at],
            device_id=to,
            device_id_type=MESH,
        )

    x_peer = dev(1 - xl, z, xh, y, c)
    w_peer = dev(1 - xl, z, 1 - xh, y, c)
    c_peer = dev(xl, z, xh, y, 1 - c)
    z_next = dev(xl, lax.rem(z + 1, 8), xh, y, c)
    z_prev = dev(xl, lax.rem(z + 7, 8), xh, y, c)

    share = y * 2 + c

    def token_rows(h):
        return pl.ds(pl.multiple_of((h * 8 + share) * TOK, TOK), TOK)

    stat_in = [
        pltpu.make_async_copy(streams[k].at[token_rows(h)], sc.at[k, h], lsem.at[k * 2 + h])
        for k in range(2)
        for h in range(2)
    ]
    stream_in_own = [pltpu.make_async_copy(streams[k], sv.at[k], lsem.at[4 + k]) for k in range(2)]
    expand_in = [pltpu.make_async_copy(expands[k], ev.at[k], lsem.at[6 + k]) for k in range(2)]
    project_in = [pltpu.make_async_copy(projects[k], pv.at[k], lsem.at[8 + k]) for k in range(2)]
    for cp in stat_in + stream_in_own[:1] + expand_in + stream_in_own[1:] + project_in:
        cp.start()

    barrier = pltpu.get_barrier_semaphore()

    def greet(d, _):
        pl.semaphore_signal(barrier, inc=1, device_id=(lax.rem(i + d, 16), j), device_id_type=MESH)
        pl.semaphore_signal(barrier, inc=1, device_id=(i, lax.rem(j + d, 16)), device_id_type=MESH)
        return 0

    lax.fori_loop(1, 16, greet, 0)
    pl.semaphore_signal(barrier, inc=1, device_id=w_peer, device_id_type=MESH)

    @pl.when(i != j)
    def _():
        pl.semaphore_signal(barrier, inc=1, device_id=(j, i), device_id_type=MESH)

    for k in range(2):
        for h in range(2):
            stat_in[k * 2 + h].wait()
            v = sc[k, h].astype(F32)
            for n, col in enumerate((v, v * v)):
                total = jnp.sum(col, axis=1, keepdims=True)
                at_row = h * 4 + k * 2 + n
                st1[at_row : at_row + 1, :] = jnp.broadcast_to(total, (TOK, TOK)).T[0:1, :]
    r1[0] = st1[...]

    @pl.when(i != j)
    def _():
        pl.semaphore_wait(barrier, 32)

    @pl.when(i == j)
    def _():
        pl.semaphore_wait(barrier, 31)

    sent, ends = [], []

    def drain():
        for cp in sent:
            cp.wait_send()
        for end in ends:
            end()

    def start(cp):
        cp.start()
        sent.append(cp)
        return cp

    def stream_copy(k):
        rows = pl.multiple_of((1 - xl) * 1024 + c * 512, 512)
        return copy(
            streams[k].at[pl.ds(rows, 512)],
            xs.at[k, pl.ds(pl.multiple_of(c * 512, 512), 512)],
            S_STREAM[k],
            w_peer,
        )

    def stream_forward(k):
        part = xs.at[k, pl.ds(pl.multiple_of(c * 512, 512), 512)]
        return copy(part, part, S_STREAM[k] + 1, c_peer)

    str_cp = [stream_copy(k) for k in range(2)]
    exp_cp = [copy(expands[k], xe.at[k], S_EXP[k], x_peer) for k in range(2)]
    prj_cp = [copy(projects[k], xp.at[k], S_PROJ[k], x_peer) for k in range(2)]
    gain_cp = [copy(gains[k], xg[k], S_GAIN[k], x_peer) for k in range(2)]
    mine = pl.ds(pl.multiple_of(j * TOK, TOK), TOK)

    def stat1(d):
        return copy(st1, r1.at[d], S_STAT1 + d, (lax.rem(i + d, 16), j))

    def stat2(d):
        return copy(st2, r2.at[share], S_STAT2 + d, (i, xh * 8 + lax.rem(share + d, 8)))

    def run(fn, lo=1, hi=16):
        def body(d, _):
            fn(d)
            return 0

        lax.fori_loop(lo, hi, body, 0)

    run(lambda d: stat1(d).start())
    ends.append(lambda: run(lambda d: stat1(d).wait_send()))
    start(gain_cp[0])
    start(gain_cp[1])
    start(str_cp[0])
    start(exp_cp[0])
    run(lambda d: stat1(d).wait_recv())
    totals = r1[0]
    for d in range(1, 16):
        totals = totals + r1[d]
    totals = totals * (1.0 / 6144.0)
    totals = jnp.where(xl == 0, totals[0:4, :], totals[4:8, :])
    st2[...] = jnp.zeros((8, TOK), F32)
    for k in range(2):
        mean = totals[2 * k : 2 * k + 1, :]
        var = totals[2 * k + 1 : 2 * k + 2, :] - mean * mean
        st2[2 * k : 2 * k + 1, :] = mean
        st2[2 * k + 1 : 2 * k + 2, :] = lax.rsqrt(var + EPS)
    r2[share] = st2[...]
    run(lambda d: stat2(d).start(), 1, 8)
    ends.append(lambda: run(lambda d: stat2(d).wait_send(), 1, 8))
    run(lambda d: stat2(d).wait_recv(), 1, 8)

    def normalise(k, part, r):
        t = xl * 8 + r
        stats = r2[r]
        mean = spread(stats[2 * k : 2 * k + 1, :])
        rstd = spread(stats[2 * k + 1 : 2 * k + 2, :])
        if part == 0:
            v = sv[k, pl.ds(pl.multiple_of(t * TOK, TOK), TOK), :]
            gain = gains[k][...]
        else:
            v = xs[k, pl.ds(pl.multiple_of(r * TOK, TOK), TOK), :]
            gain = xg[k][...]
        mean, rstd = (jnp.concatenate([q, q, q], axis=1) for q in (mean, rstd))
        nrm[k, r, part] = ((v.astype(F32) - mean) * rstd * gain.reshape(1, W)).astype(BF16)

    def stream_in(k):
        str_cp[k].wait_recv()
        start(stream_forward(k))

    gain_cp[0].wait_recv()
    gain_cp[1].wait_recv()
    stream_in_own[0].wait()
    run(lambda r: normalise(0, 0, r), 0, 8)
    stream_in(0)
    start(str_cp[1])
    stream_forward(0).wait_recv()
    run(lambda r: normalise(0, 1, r), 0, 8)
    exp_cp[0].wait_recv()
    start(exp_cp[1])
    expand_in[0].wait()
    stream_in_own[1].wait()

    def cols(h):
        return slice(h * W, (h + 1) * W)

    def partial_pre(k, r, h):
        own = jnp.dot(nrm[k, r, 0], ev[k, :, cols(h)], preferred_element_type=F32)
        return own + jnp.dot(nrm[k, r, 1], xe[k, :, cols(h)], preferred_element_type=F32)

    def part(ref, u):
        return ref.at[pl.ds(u * 64, 64)]

    def rs_copy(k, s, h, u):
        sem = S_RS[k] + 4 * s + 2 * h + u
        return copy(part(rsb.at[k, s, h], u), part(rr.at[k, s, h], u), sem, (z_next, z_prev)[h])

    def rs_step(k, s, first=False):
        own = [
            partial_pre(k, lax.rem(z + 7 - s + 8, 8) if h == 0 else lax.rem(z + 1 + s, 8), h)
            for h in range(2)
        ]
        for u in range(2):
            rows = slice(u * 64, (u + 1) * 64)
            for h in range(2):
                acc = own[h][rows]
                if not first:
                    rs_copy(k, s - 1, h, u).wait_recv()
                    acc = acc + rr[k, s - 1, h, rows].astype(F32)
                rsb[k, s, h, rows] = acc.astype(BF16)
                rs_copy(k, s, h, u).start()

    def rs_sent(k):
        for h in range(2):
            for u in range(2):
                run(lambda s: rs_copy(k, s, h, u).wait_send(), 0, 7)

    def rs_finish(k):
        for h in range(2):
            acc = partial_pre(k, z, h) + shifts[k][cols(h)].reshape(1, W)
            for u in range(2):
                rs_copy(k, 6, h, u).wait_recv()
            acc = acc + rr[k, 6, h].astype(F32)
            act[k, z, h] = (0.5 * acc * (1.0 + lax.erf(acc * (0.5 ** 0.5)))).astype(BF16)

    def ag_copy(k, s, way, half):
        if way == 0:
            r, to = lax.rem(z - s + 8, 8), z_next
        else:
            r, to = lax.rem(z + s, 8), z_prev
        ref = act.at[k, r, half]
        return copy(ref, ref, S_AG[k] + 4 * s + 2 * way + half, to)

    def ag_step(k, s, first=False, last=False):
        for half in range(2):
            for way in range(2):
                if not first:
                    ag_copy(k, s - 1, way, half).wait_recv()
                if not last or half == way:
                    ag_copy(k, s, way, half).start()

    def ag_finish(k):
        for way in range(2):
            ag_copy(k, 3, way, way).wait_recv()

    def ag_sent(k):
        for way in range(2):
            for half in range(2):
                run(lambda s: ag_copy(k, s, way, half).wait_send(), 0, 3)
            ag_copy(k, 3, way, way).wait_send()

    def gemm2(k, r):
        for b, weight in enumerate((pv.at[k], xp.at[k])):
            out = jnp.dot(act[k, r, 0], weight[0:W, :], preferred_element_type=F32)
            out = out + jnp.dot(act[k, r, 1], weight[W:HID, :], preferred_element_type=F32)
            yb[k, lax.rem(r, 2), lax.div(r, 2), b] = out.astype(BF16)

    def core_copy(k):
        return copy(yb.at[k, 1 - c], cr.at[k], S_CORE[k], c_peer)

    def y_copy(k, d):
        return copy(ys.at[k, d - 1], yr.at[k, d - 1], S_Y[k] + d, dev(xl, z, xh, lax.rem(y + d, 4), c))

    def chip_sum(k, t):
        return yb[k, c, t].astype(F32) + cr[k, t].astype(F32)

    def y_start(k):
        core_copy(k).wait_recv()
        for d in (2, 1, 3):
            ys[k, d - 1] = chip_sum(k, lax.rem(y + d, 4)).astype(BF16)
            start(y_copy(k, d))

    def x_copy_a(k):
        return copy(
            xt.at[k, 1], xr.at[k, xh], S_X[k], dev(1 - xl, z, xl, y, c), S_X[k] + xh
        )

    def x_copy_a_in(k, n):
        return copy(xt.at[k, 1], xr.at[k, n], S_X[k], x_peer, S_X[k] + n)

    def x_copy_b(k):
        return copy(xt.at[k, 0], xr.at[k, 2], S_X[k] + 2, dev(xl, z, 1 - xh, y, c))

    def x_start(k):
        total = chip_sum(k, y)
        for d in (1, 3, 2):
            y_copy(k, d).wait_recv()
            total = total + yr[k, d - 1].astype(F32)
        xt[k] = total.astype(BF16)
        start(x_copy_a(k))

        @pl.when(xh != xl)
        def _():
            x_copy_b(k).start()

    def finish(k):
        def put(branch):
            resid = sv[k, mine, :].astype(F32) + offsets[k][...].reshape(1, W)
            afters[k][...] = (resid + branch).astype(BF16)

        @pl.when(xh != xl)
        def _():
            x_copy_a_in(k, 0).wait_recv()
            x_copy_a_in(k, 1).wait_recv()
            put(xr[k, 0].astype(F32) + xr[k, 1].astype(F32))
            x_copy_b(k).wait_send()

        @pl.when(xh == xl)
        def _():
            x_copy_b(k).wait_recv()
            put(xt[k, 0].astype(F32) + xr[k, 2].astype(F32))

    rs_step(0, 0, True)

    def own_part(s):
        rs_step(0, s)
        normalise(1, 0, 2 * s - 2)
        normalise(1, 0, 2 * s - 1)

    run(own_part, 1, 5)
    stream_in(1)
    exp_cp[1].wait_recv()
    start(prj_cp[0])
    start(prj_cp[1])
    expand_in[1].wait()
    stream_forward(1).wait_recv()

    def peer_part(s):
        rs_step(0, s)
        run(lambda n: normalise(1, 1, 4 * (s - 5) + n), 0, 4)

    run(peer_part, 5, 7)
    ends.append(lambda: rs_sent(0))

    rs_step(1, 0, True)
    rs_finish(0)
    ag_step(0, 0, True)

    def both(q, _):
        rs_step(1, 2 * q + 1)
        ag_step(0, q + 1)
        rs_step(1, 2 * q + 2)
        return 0

    lax.fori_loop(0, 2, both, 0)
    rs_step(1, 5)
    ag_step(0, 3, last=True)
    rs_step(1, 6)
    ends.append(lambda: rs_sent(1))
    ends.append(lambda: ag_sent(0))
    rs_finish(1)

    def gemm2_pair(k, s):
        gemm2(k, lax.rem(z - s + 8, 8))
        gemm2(k, lax.rem(z + s, 8))

    ag_step(1, 0, True)
    ag_finish(0)
    project_in[0].wait()
    project_in[1].wait()
    prj_cp[0].wait_recv()
    run(lambda r: gemm2(0, r), 0, 8)
    start(core_copy(0))
    ag_step(1, 1)
    y_start(0)
    prj_cp[1].wait_recv()
    gemm2(1, z)
    gemm2_pair(1, 1)
    ag_step(1, 2)
    gemm2_pair(1, 2)
    ag_step(1, 3, last=True)
    x_start(0)
    gemm2_pair(1, 3)
    ag_finish(1)
    ends.append(lambda: ag_sent(1))
    gemm2(1, lax.rem(z + 4, 8))
    start(core_copy(1))
    finish(0)

    place = xh * 4 + y
    y_start(1)
    al[share, xh] = a_l[...]

    def left_copy(d):
        to = lax.rem(place + d, 8)
        return copy(a_l, al.at[share, xh], S_LEFT + d, (i, to * 2 + c))

    def left_forward(d):
        came = lax.rem(place - d + 8, 8)
        ref = al.at[lax.rem(came, 4) * 2 + c, lax.div(came, 4)]
        return copy(ref, ref, S_LEFTC + d, c_peer)

    run(lambda d: left_copy(d).start(), 1, 8)
    left_forward(0).start()
    ends.append(lambda: run(lambda d: left_copy(d).wait_send(), 1, 8))
    ends.append(lambda: run(lambda d: left_forward(d).wait_send(), 0, 8))
    x_start(1)
    finish(1)

    turn = copy(a_r, at.at[lax.rem(j, 8), lax.div(j, 8)], S_TURN, (j, i))

    @pl.when(i != j)
    def _():
        turn.start()

    @pl.when(i == j)
    def _():
        at[z, xl] = a_r[...]

    def left_pass(d):
        left_copy(d).wait_recv()
        left_forward(d).start()

    run(left_pass, 1, 8)

    @pl.when(i != j)
    def _():
        turn.wait()

    here = at.at[z, xl]
    pair = start(copy(here, here, S_PAIR, x_peer))

    def right_copy(s, way, which):
        if way == 0:
            r, to = lax.rem(z - s + 8, 8), z_next
        else:
            r, to = lax.rem(z + s, 8), z_prev
        ref = at.at[r, xl if which == 0 else 1 - xl]
        return copy(ref, ref, S_RIGHT + 4 * s + 2 * way + which, to)

    def add(r, first=False):
        term = lax.dot_general(
            al[r].reshape(2 * TOK, W),
            at[r].reshape(2 * TOK, W),
            (((0,), (0,)), ((), ())),
            preferred_element_type=F32,
        )
        corr[...] = term if first else corr[...] + term

    for way in range(2):
        start(right_copy(0, way, 0))
    pair.wait_recv()
    for way in range(2):
        start(right_copy(0, way, 1))
    run(lambda d: left_forward(d).wait_recv(), 0, 8)
    add(z, True)
    for s in range(1, 4):
        for which in range(2):
            for way in range(2):
                right_copy(s - 1, way, which).wait_recv()
                if s < 3 or way == which:
                    start(right_copy(s, way, which))
        add(lax.rem(z - s + 8, 8))
        add(lax.rem(z + s, 8))
    for way in range(2):
        right_copy(3, way, way).wait_recv()
    add(lax.rem(z + 4, 8))
    corr[...] = corr[...] * (1.0 / 2048.0)
    drain()


def hand_out(a_l, a_r, corr, a_l_out, a_r_out, corr_out, sems):
    copies = [
        pltpu.make_async_copy(src, dst, sems.at[n])
        for n, (src, dst) in enumerate(((corr, corr_out), (a_l, a_l_out), (a_r, a_r_out)))
    ]
    for cp in copies:
        cp.start()
    for cp in copies:
        cp.wait()


def per_device(s_l, s_r, g_l, g_r, e_l, e_r, b_l, b_r, p_l, p_r, o_l, o_r):
    vm = pl.BlockSpec(memory_space=pltpu.VMEM)
    hbm = pl.BlockSpec(memory_space=pl.ANY)
    tile = (TOK, W)
    shapes = (
        jax.ShapeDtypeStruct(tile, BF16),
        jax.ShapeDtypeStruct(tile, BF16),
        jax.ShapeDtypeStruct((W, W), F32),
    )
    results = pl.pallas_call(
        kernel,
        out_shape=shapes,
        in_specs=[hbm, hbm, vm, vm, hbm, hbm, vm, vm, hbm, hbm, vm, vm],
        out_specs=(vm, vm, vm),
        scratch_shapes=[
            pltpu.VMEM((8, TOK), F32),
            pltpu.VMEM((8, TOK), F32),
            pltpu.VMEM((16, 8, TOK), F32),
            pltpu.VMEM((8, 8, TOK), F32),
            pltpu.VMEM((2, W, HID), BF16),
            pltpu.VMEM((2, HID, W), BF16),
            pltpu.VMEM((W,), F32),
            pltpu.VMEM((W,), F32),
            pltpu.VMEM((2, 1024, W), BF16),
            pltpu.VMEM((2, 8, 2) + tile, BF16),
            pltpu.VMEM((2, 7, 2) + tile, BF16),
            pltpu.VMEM((2, 7, 2) + tile, BF16),
            pltpu.VMEM((2, 8, 2) + tile, BF16),
            pltpu.VMEM((2, 2, 4, 2) + tile, BF16),
            pltpu.VMEM((2, 4, 2) + tile, BF16),
            pltpu.VMEM((2, 3, 2) + tile, BF16),
            pltpu.VMEM((2, 3, 2) + tile, BF16),
            pltpu.VMEM((2, 2) + tile, BF16),
            pltpu.VMEM((2, 3) + tile, BF16),
            pltpu.VMEM((8, 2) + tile, BF16),
            pltpu.VMEM((8, 2) + tile, BF16),
            pltpu.VMEM((2, 2) + tile, BF16),
            pltpu.VMEM((2, 2048, W), BF16),
            pltpu.VMEM((2, W, HID), BF16),
            pltpu.VMEM((2, HID, W), BF16),
            pltpu.SemaphoreType.DMA((N_SEMS,)),
            pltpu.SemaphoreType.DMA((N_SEMS,)),
            pltpu.SemaphoreType.DMA((10,)),
        ],
        compiler_params=pltpu.CompilerParams(
            collective_id=0, has_side_effects=True, vmem_limit_bytes=56 * 1024 * 1024
        ),
    )(s_l, s_r, g_l, g_r, e_l, e_r, b_l, b_r, p_l, p_r, o_l, o_r)
    return pl.pallas_call(
        hand_out,
        out_shape=shapes,
        in_specs=[hbm] * 3,
        out_specs=(hbm,) * 3,
        scratch_shapes=[pltpu.SemaphoreType.DMA((3,))],
    )(*results)


def solution(mesh):
    placed = (
        P(None, "dp"),
        P(None, "dp"),
        P("dp"),
        P("dp"),
        P("dp", "mp"),
        P("dp", "mp"),
        P("mp"),
        P("mp"),
        P("mp", "dp"),
        P("mp", "dp"),
        P("dp"),
        P("dp"),
    )
    return jax.shard_map(
        per_device,
        mesh=mesh,
        in_specs=placed,
        out_specs=(P("mp", "dp"), P("mp", "dp"), P("dp", "mp")),
        check_vma=False,
    )
```

time: 204 us -> 189 us (0.926)
  local copies, waits for them, and re-layouts: 12.6 us -> 0 us
    reshape x6 -> x0, local copies, waits for them, and re-layouts: 7.55 us -> none  [per_device(): row = lambda v: v.reshape(1, -1)]
    unnamed x3 -> x0, local copies, waits for them, and re-layouts: 5 us -> none
    pallas_call x1 -> x2, Pallas kernels: 187 us -> 186 us  [the longest x1 161 us: per_device(): pl.pallas_call(kernel, out_shape=shapes, in_specs=[hbm, hbm, vm, vm, hbm,...]
where the time goes in v2:
time: 189 us; the launch traced here: 186 us
  Pallas kernels  186 us (98%)
    pallas_call x1, Pallas kernels, per_device(): pl.pallas_call(kernel, out_shape=shapes, in_specs=[hbm, hbm, vm, vm, hbm,...  161 us
    pallas_call x1, Pallas kernels, per_device(): pl.pallas_call(hand_out, out_shape=shapes, in_specs=[hbm] * 3, out_specs=...  25 us

profile of v2, /device:TPU:32, one launch (start us, length us, event | category | flops | bytes accessed | tf_op | source)
XLA Modules:
  0.0 186.3 jit_solution(15723973653221402252)
XLA Ops:
  0.6 160.7 %shard_map.139 = (bf16[128,384]{1,0:T(8,128)(2,1)}, bf16[128,384]{1,0:T(8,128)(2,1)}, f32[384,384]{1,0:T(8,128)}) custom-call(bf16[2048,384]{1,0:T(8,128)(2,1)} %s_l.1, bf16[2048,384]{1,0:T(8,128)(2,1)} %s_r.1, f32[384]{0:T(512)} %g_l.1, f32[384]{0:T(512)} %g_r.1, bf16[384,768]{1,0:T(8,128)(2,1)} %e_l.1, bf16[384,768]{1,0:T(8,128)(2,1)} %e_r.1, f32[768]{0:T(1024)} %b_l.1, ...), custom_call_target="tpu_custom_call" | custom-call | tf_op jit(solution)/shard_map/pallas_call | solution.py:531
  161.3 25.0 %shard_map.140 = (bf16[128,384]{1,0:T(8,128)(2,1)}, bf16[128,384]{1,0:T(8,128)(2,1)}, f32[384,384]{1,0:T(8,128)}) custom-call(bf16[128,384]{1,0:T(8,128)(2,1)} %get-tuple-element.6.a_l, bf16[128,384]{1,0:T(8,128)(2,1)} %get-tuple-element.7.a_r, f32[384,384]{1,0:T(8,128)} %get-tuple-element.8.corr), custom_call_target="tpu_custom_call" | custom-call | tf_op jit(solution)/shard_map/pallas_call | solution.py:570

commit v3 on v2

--- a/solution.py
+++ b/solution.py
@@ -31,11 +31,11 @@
 SLOTS = Slots()
 S_STAT1 = SLOTS.take(16)
 S_STAT2 = SLOTS.take(16)
-S_EXP = [SLOTS.take(1) for _ in range(2)]
+S_EXP = [SLOTS.take(2) for _ in range(2)]
 S_PROJ = [SLOTS.take(1) for _ in range(2)]
 S_GAIN = [SLOTS.take(1) for _ in range(2)]
-S_STREAM = [SLOTS.take(2) for _ in range(2)]
-S_RS = [SLOTS.take(28) for _ in range(2)]
+S_STREAM = [SLOTS.take(16) for _ in range(2)]
+S_RS = [SLOTS.take(16) for _ in range(2)]
 S_AG = [SLOTS.take(16) for _ in range(2)]
 S_CORE = [SLOTS.take(1) for _ in range(2)]
 S_Y = [SLOTS.take(4) for _ in range(2)]
@@ -144,21 +144,29 @@
         sent.append(cp)
         return cp
 
-    def stream_copy(k):
-        rows = pl.multiple_of((1 - xl) * 1024 + c * 512, 512)
+    def nth_chunk(n):
+        return lax.rem(z + 4 + (1 - 2 * lax.rem(n, 2)) * lax.div(n + 1, 2) + 8, 8)
+
+    half_rows = pl.ds(pl.multiple_of(c * 64, 64), 64)
+
+    def stream_copy(k, n):
+        r = nth_chunk(n)
+        rows = pl.multiple_of(((1 - xl) * 8 + r) * TOK + c * 64, 64)
         return copy(
-            streams[k].at[pl.ds(rows, 512)],
-            xs.at[k, pl.ds(pl.multiple_of(c * 512, 512), 512)],
-            S_STREAM[k],
-            w_peer,
+            streams[k].at[pl.ds(rows, 64)], xs.at[k, r, half_rows], S_STREAM[k] + n, w_peer
         )
 
-    def stream_forward(k):
-        part = xs.at[k, pl.ds(pl.multiple_of(c * 512, 512), 512)]
-        return copy(part, part, S_STREAM[k] + 1, c_peer)
-
-    str_cp = [stream_copy(k) for k in range(2)]
-    exp_cp = [copy(expands[k], xe.at[k], S_EXP[k], x_peer) for k in range(2)]
+    def stream_forward(k, n):
+        piece = xs.at[k, nth_chunk(n), half_rows]
+        return copy(piece, piece, S_STREAM[k] + 8 + n, c_peer)
+
+    def cols(h):
+        return slice(h * W, (h + 1) * W)
+
+    exp_cp = [
+        [copy(expands[k].at[:, cols(h)], xe.at[k, h], S_EXP[k] + h, x_peer) for h in range(2)]
+        for k in range(2)
+    ]
     prj_cp = [copy(projects[k], xp.at[k], S_PROJ[k], x_peer) for k in range(2)]
     gain_cp = [copy(gains[k], xg[k], S_GAIN[k], x_peer) for k in range(2)]
     mine = pl.ds(pl.multiple_of(j * TOK, TOK), TOK)
@@ -180,8 +188,9 @@
     ends.append(lambda: run(lambda d: stat1(d).wait_send()))
     start(gain_cp[0])
     start(gain_cp[1])
-    start(str_cp[0])
-    start(exp_cp[0])
+    start(exp_cp[0][0])
+    run(lambda n: stream_copy(0, n).start(), 0, 8)
+    start(exp_cp[0][1])
     run(lambda d: stat1(d).wait_recv())
     totals = r1[0]
     for d in range(1, 16):
@@ -208,69 +217,58 @@
             v = sv[k, pl.ds(pl.multiple_of(t * TOK, TOK), TOK), :]
             gain = gains[k][...]
         else:
-            v = xs[k, pl.ds(pl.multiple_of(r * TOK, TOK), TOK), :]
+            v = xs[k, r]
             gain = xg[k][...]
         mean, rstd = (jnp.concatenate([q, q, q], axis=1) for q in (mean, rstd))
         nrm[k, r, part] = ((v.astype(F32) - mean) * rstd * gain.reshape(1, W)).astype(BF16)
 
-    def stream_in(k):
-        str_cp[k].wait_recv()
-        start(stream_forward(k))
-
-    gain_cp[0].wait_recv()
-    gain_cp[1].wait_recv()
-    stream_in_own[0].wait()
-    run(lambda r: normalise(0, 0, r), 0, 8)
-    stream_in(0)
-    start(str_cp[1])
-    stream_forward(0).wait_recv()
-    run(lambda r: normalise(0, 1, r), 0, 8)
-    exp_cp[0].wait_recv()
-    start(exp_cp[1])
-    expand_in[0].wait()
-    stream_in_own[1].wait()
-
-    def cols(h):
-        return slice(h * W, (h + 1) * W)
+    def pass_on(k, lo, hi):
+        def one(n):
+            stream_copy(k, n).wait_recv()
+            stream_forward(k, n).start()
+
+        run(one, lo, hi)
+
+    def prepare(k, lo, hi):
+        def one(n):
+            stream_forward(k, n).wait_recv()
+            normalise(k, 1, nth_chunk(n))
+
+        run(one, lo, hi)
 
     def partial_pre(k, r, h):
         own = jnp.dot(nrm[k, r, 0], ev[k, :, cols(h)], preferred_element_type=F32)
-        return own + jnp.dot(nrm[k, r, 1], xe[k, :, cols(h)], preferred_element_type=F32)
-
-    def part(ref, u):
-        return ref.at[pl.ds(u * 64, 64)]
-
-    def rs_copy(k, s, h, u):
-        sem = S_RS[k] + 4 * s + 2 * h + u
-        return copy(part(rsb.at[k, s, h], u), part(rr.at[k, s, h], u), sem, (z_next, z_prev)[h])
-
-    def rs_step(k, s, first=False):
-        own = [
-            partial_pre(k, lax.rem(z + 7 - s + 8, 8) if h == 0 else lax.rem(z + 1 + s, 8), h)
-            for h in range(2)
-        ]
-        for u in range(2):
-            rows = slice(u * 64, (u + 1) * 64)
-            for h in range(2):
-                acc = own[h][rows]
-                if not first:
-                    rs_copy(k, s - 1, h, u).wait_recv()
-                    acc = acc + rr[k, s - 1, h, rows].astype(F32)
-                rsb[k, s, h, rows] = acc.astype(BF16)
-                rs_copy(k, s, h, u).start()
+        return own + jnp.dot(nrm[k, r, 1], xe[k, h], preferred_element_type=F32)
+
+    def rs_copy(k, s, way, half):
+        sem = S_RS[k] + 4 * s + 2 * way + half
+        return copy(rsb.at[k, s, way, half], rr.at[k, s, way, half], sem, (z_next, z_prev)[way])
+
+    def rs_step(k, s, half):
+        for way in range(2):
+            if s == 0 and half != way:
+                continue
+            r = lax.rem(z + 4 - s + 8, 8) if way == 0 else lax.rem(z + 4 + s, 8)
+            acc = partial_pre(k, r, half)
+            if s > 1 or (s == 1 and half == way):
+                rs_copy(k, s - 1, way, half).wait_recv()
+                acc = acc + rr[k, s - 1, way, half].astype(F32)
+            rsb[k, s, way, half] = acc.astype(BF16)
+            rs_copy(k, s, way, half).start()
 
     def rs_sent(k):
-        for h in range(2):
-            for u in range(2):
-                run(lambda s: rs_copy(k, s, h, u).wait_send(), 0, 7)
+        for way in range(2):
+            rs_copy(k, 0, way, way).wait_send()
+            for half in range(2):
+                run(lambda s: rs_copy(k, s, way, half).wait_send(), 1, 4)
 
     def rs_finish(k):
-        for h in range(2):
-            acc = partial_pre(k, z, h) + shifts[k][cols(h)].reshape(1, W)
-            for u in range(2):
-                rs_copy(k, 6, h, u).wait_recv()
-            acc = acc + rr[k, 6, h].astype(F32)
-            act[k, z, h] = (0.5 * acc * (1.0 + lax.erf(acc * (0.5 ** 0.5)))).astype(BF16)
+        for half in range(2):
+            acc = partial_pre(k, z, half) + shifts[k][cols(half)].reshape(1, W)
+            for way in range(2):
+                rs_copy(k, 3, way, half).wait_recv()
+                acc = acc + rr[k, 3, way, half].astype(F32)
+            act[k, z, half] = (0.5 * acc * (1.0 + lax.erf(acc * (0.5 ** 0.5)))).astype(BF16)
 
     def ag_copy(k, s, way, half):
         if way == 0:
@@ -359,42 +357,52 @@
             x_copy_b(k).wait_recv()
             put(xt[k, 0].astype(F32) + xr[k, 2].astype(F32))
 
-    rs_step(0, 0, True)
-
-    def own_part(s):
-        rs_step(0, s)
-        normalise(1, 0, 2 * s - 2)
-        normalise(1, 0, 2 * s - 1)
-
-    run(own_part, 1, 5)
-    stream_in(1)
-    exp_cp[1].wait_recv()
-    start(prj_cp[0])
-    start(prj_cp[1])
-    expand_in[1].wait()
-    stream_forward(1).wait_recv()
-
-    def peer_part(s):
-        rs_step(0, s)
-        run(lambda n: normalise(1, 1, 4 * (s - 5) + n), 0, 4)
-
-    run(peer_part, 5, 7)
+    gain_cp[0].wait_recv()
+    gain_cp[1].wait_recv()
+    stream_in_own[0].wait()
+    expand_in[0].wait()
+    pass_on(0, 0, 3)
+    run(lambda r: normalise(0, 0, r), 0, 8)
+    prepare(0, 0, 3)
+    exp_cp[0][0].wait_recv()
+    rs_step(0, 0, 0)
+    pass_on(0, 3, 8)
+    run(lambda n: stream_copy(1, n).start(), 0, 8)
+    rs_step(0, 1, 0)
+    prepare(0, 3, 5)
+    exp_cp[0][1].wait_recv()
+    start(exp_cp[1][0])
+    start(exp_cp[1][1])
+    rs_step(0, 0, 1)
+    rs_step(0, 2, 0)
+    prepare(0, 5, 8)
+    rs_step(0, 1, 1)
+    rs_step(0, 3, 0)
+    stream_in_own[1].wait()
+    run(lambda r: normalise(1, 0, r), 0, 8)
+    rs_step(0, 2, 1)
+    pass_on(1, 0, 8)
+    rs_step(0, 3, 1)
+    prepare(1, 0, 8)
+    for k in range(2):
+        ends.append(lambda k=k: run(lambda n: stream_copy(k, n).wait_send(), 0, 8))
+        ends.append(lambda k=k: run(lambda n: stream_forward(k, n).wait_send(), 0, 8))
     ends.append(lambda: rs_sent(0))
 
-    rs_step(1, 0, True)
     rs_finish(0)
     ag_step(0, 0, True)
-
-    def both(q, _):
-        rs_step(1, 2 * q + 1)
-        ag_step(0, q + 1)
-        rs_step(1, 2 * q + 2)
-        return 0
-
-    lax.fori_loop(0, 2, both, 0)
-    rs_step(1, 5)
-    ag_step(0, 3, last=True)
-    rs_step(1, 6)
+    expand_in[1].wait()
+    exp_cp[1][0].wait_recv()
+    rs_step(1, 0, 0)
+    exp_cp[1][1].wait_recv()
+    start(prj_cp[0])
+    rs_step(1, 0, 1)
+    for s in range(1, 4):
+        ag_step(0, s, last=s == 3)
+        rs_step(1, s, 0)
+        rs_step(1, s, 1)
+        if s == 2:
+            start(prj_cp[1])
     ends.append(lambda: rs_sent(1))
     ends.append(lambda: ag_sent(0))
     rs_finish(1)
@@ -439,28 +447,27 @@
         ref = al.at[lax.rem(came, 4) * 2 + c, lax.div(came, 4)]
         return copy(ref, ref, S_LEFTC + d, c_peer)
 
+    x_start(1)
+    finish(1)
+
+    turn = copy(a_r, at.at[lax.rem(j, 8), lax.div(j, 8)], S_TURN, (j, i))
+
+    @pl.when(i != j)
+    def _():
+        turn.start()
+
+    @pl.when(i == j)
+    def _():
+        at[z, xl] = a_r[...]
+
     run(lambda d: left_copy(d).start(), 1, 8)
     left_forward(0).start()
     ends.append(lambda: run(lambda d: left_copy(d).wait_send(), 1, 8))
     ends.append(lambda: run(lambda d: left_forward(d).wait_send(), 0, 8))
-    x_start(1)
-    finish(1)
-
-    turn = copy(a_r, at.at[lax.rem(j, 8), lax.div(j, 8)], S_TURN, (j, i))
-
-    @pl.when(i != j)
-    def _():
-        turn.start()
-
-    @pl.when(i == j)
-    def _():
-        at[z, xl] = a_r[...]
 
     def left_pass(d):
         left_copy(d).wait_recv()
         left_forward(d).start()
-
-    run(left_pass, 1, 8)
 
     @pl.when(i != j)
     def _():
@@ -486,37 +493,42 @@
         )
         corr[...] = term if first else corr[...] + term
 
+    def pass_right(s):
+        for which in range(2):
+            for way in range(2):
+                right_copy(s - 1, way, which).wait_recv()
+                if s < 3 or way == which:
+                    start(right_copy(s, way, which))
+
+    def add_pair(s):
+        add(lax.rem(z - s + 8, 8))
+        add(lax.rem(z + s, 8))
+
     for way in range(2):
         start(right_copy(0, way, 0))
     pair.wait_recv()
     for way in range(2):
         start(right_copy(0, way, 1))
+    run(left_pass, 1, 4)
+    pass_right(1)
+    run(left_pass, 4, 8)
+    pass_right(2)
     run(lambda d: left_forward(d).wait_recv(), 0, 8)
     add(z, True)
-    for s in range(1, 4):
-        for which in range(2):
-            for way in range(2):
-                right_copy(s - 1, way, which).wait_recv()
-                if s < 3 or way == which:
-                    start(right_copy(s, way, which))
-        add(lax.rem(z - s + 8, 8))
-        add(lax.rem(z + s, 8))
+    add_pair(1)
+    pass_right(3)
+    add_pair(2)
+    add_pair(3)
     for way in range(2):
         right_copy(3, way, way).wait_recv()
     add(lax.rem(z + 4, 8))
-    corr[...] = corr[...] * (1.0 / 2048.0)
     drain()
 
 
-def hand_out(a_l, a_r, corr, a_l_out, a_r_out, corr_out, sems):
-    copies = [
-        pltpu.make_async_copy(src, dst, sems.at[n])
-        for n, (src, dst) in enumerate(((corr, corr_out), (a_l, a_l_out), (a_r, a_r_out)))
-    ]
-    for cp in copies:
-        cp.start()
-    for cp in copies:
-        cp.wait()
+def hand_out(a_l, a_r, corr, a_l_out, a_r_out, corr_out):
+    a_l_out[...] = a_l[...]
+    a_r_out[...] = a_r[...]
+    corr_out[...] = corr[...] * (1.0 / 2048.0)
 
 
 def per_device(s_l, s_r, g_l, g_r, e_l, e_r, b_l, b_r, p_l, p_r, o_l, o_r):
@@ -538,14 +550,14 @@
             pltpu.VMEM((8, TOK), F32),
             pltpu.VMEM((16, 8, TOK), F32),
             pltpu.VMEM((8, 8, TOK), F32),
-            pltpu.VMEM((2, W, HID), BF16),
+            pltpu.VMEM((2, 2, W, W), BF16),
             pltpu.VMEM((2, HID, W), BF16),
             pltpu.VMEM((W,), F32),
             pltpu.VMEM((W,), F32),
-            pltpu.VMEM((2, 1024, W), BF16),
+            pltpu.VMEM((2, 8) + tile, BF16),
             pltpu.VMEM((2, 8, 2) + tile, BF16),
-            pltpu.VMEM((2, 7, 2) + tile, BF16),
-            pltpu.VMEM((2, 7, 2) + tile, BF16),
+            pltpu.VMEM((2, 4, 2, 2) + tile, BF16),
+            pltpu.VMEM((2, 4, 2, 2) + tile, BF16),
             pltpu.VMEM((2, 8, 2) + tile, BF16),
             pltpu.VMEM((2, 2, 4, 2) + tile, BF16),
             pltpu.VMEM((2, 4, 2) + tile, BF16),
@@ -570,9 +582,8 @@
     return pl.pallas_call(
         hand_out,
         out_shape=shapes,
-        in_specs=[hbm] * 3,
-        out_specs=(hbm,) * 3,
-        scratch_shapes=[pltpu.SemaphoreType.DMA((3,))],
+        in_specs=[vm] * 3,
+        out_specs=(vm,) * 3,
     )(*results)
 
 

time: 189 us -> 162 us (0.86)
  the two profiles are of different devices: /device:TPU:32 before, /device:TPU:40 now
where the time goes in v3:
time: 162 us
  Pallas kernels  161 us (99%)
    pallas_call x1, Pallas kernels, per_device(): pl.pallas_call(kernel, out_shape=shapes, in_specs=[hbm, hbm, vm, vm, hbm,...  159 us

profile of v3, /device:TPU:40, one launch (start us, length us, event | category | flops | bytes accessed | tf_op | source)
XLA Modules:
  0.0 162.0 jit_solution(11769273751696358517)
XLA Ops:
  0.6 159.3 %shard_map.139 = (bf16[128,384]{1,0:T(8,128)(2,1)}, bf16[128,384]{1,0:T(8,128)(2,1)}, f32[384,384]{1,0:T(8,128)}) custom-call(bf16[2048,384]{1,0:T(8,128)(2,1)} %s_l.1, bf16[2048,384]{1,0:T(8,128)(2,1)} %s_r.1, f32[384]{0:T(512)} %g_l.1, f32[384]{0:T(512)} %g_r.1, bf16[384,768]{1,0:T(8,128)(2,1)} %e_l.1, bf16[384,768]{1,0:T(8,128)(2,1)} %e_r.1, f32[768]{0:T(1024)} %b_l.1, ...), custom_call_target="tpu_custom_call" | custom-call | tf_op jit(solution)/shard_map/pallas_call | solution.py:543
  160.0 2.1 %shard_map.140 = (bf16[128,384]{1,0:T(8,128)(2,1)}, bf16[128,384]{1,0:T(8,128)(2,1)}, f32[384,384]{1,0:T(8,128)}) custom-call(bf16[128,384]{1,0:T(8,128)(2,1)} %get-tuple-element.6.a_l, bf16[128,384]{1,0:T(8,128)(2,1)} %get-tuple-element.7.a_r, f32[384,384]{1,0:T(8,128)} %get-tuple-element.8.corr), custom_call_target="tpu_custom_call" | custom-call | tf_op jit(solution)/shard_map/pallas_call | solution.py:582

commit v4 on v3

--- a/solution.py
+++ b/solution.py
@@ -37,14 +37,15 @@
 S_STREAM = [SLOTS.take(16) for _ in range(2)]
 S_RS = [SLOTS.take(16) for _ in range(2)]
 S_AG = [SLOTS.take(16) for _ in range(2)]
-S_CORE = [SLOTS.take(1) for _ in range(2)]
-S_Y = [SLOTS.take(4) for _ in range(2)]
+S_CORE = [SLOTS.take(2) for _ in range(2)]
+S_Y = [SLOTS.take(8) for _ in range(2)]
 S_X = [SLOTS.take(3) for _ in range(2)]
 S_LEFT = SLOTS.take(8)
 S_LEFTC = SLOTS.take(8)
 S_TURN = SLOTS.take(1)
 S_PAIR = SLOTS.take(1)
 S_RIGHT = SLOTS.take(16)
+S_CROSS = SLOTS.take(3)
 N_SEMS = SLOTS.count
 
 
@@ -300,22 +301,28 @@
         for b, weight in enumerate((pv.at[k], xp.at[k])):
             out = jnp.dot(act[k, r, 0], weight[0:W, :], preferred_element_type=F32)
             out = out + jnp.dot(act[k, r, 1], weight[W:HID, :], preferred_element_type=F32)
-            yb[k, lax.rem(r, 2), lax.div(r, 2), b] = out.astype(BF16)
-
-    def core_copy(k):
-        return copy(yb.at[k, 1 - c], cr.at[k], S_CORE[k], c_peer)
-
-    def y_copy(k, d):
-        return copy(ys.at[k, d - 1], yr.at[k, d - 1], S_Y[k] + d, dev(xl, z, xh, lax.rem(y + d, 4), c))
-
-    def chip_sum(k, t):
-        return yb[k, c, t].astype(F32) + cr[k, t].astype(F32)
+            yb[k, lax.rem(r, 2), b, lax.div(r, 2)] = out.astype(BF16)
+
+    def core_copy(k, b):
+        return copy(yb.at[k, 1 - c, b], cr.at[k, b], S_CORE[k] + b, c_peer)
+
+    def core_start(k):
+        for b in (1, 0):
+            start(core_copy(k, b))
+
+    def y_copy(k, d, b):
+        to = dev(xl, z, xh, lax.rem(y + d, 4), c)
+        return copy(ys.at[k, d - 1, b], yr.at[k, d - 1, b], S_Y[k] + 2 * d + b, to)
+
+    def chip_sum(k, t, b):
+        return yb[k, c, b, t].astype(F32) + cr[k, b, t].astype(F32)
 
     def y_start(k):
-        core_copy(k).wait_recv()
-        for d in (2, 1, 3):
-            ys[k, d - 1] = chip_sum(k, lax.rem(y + d, 4)).astype(BF16)
-            start(y_copy(k, d))
+        for b in (1, 0):
+            core_copy(k, b).wait_recv()
+            for d in (2, 1, 3):
+                ys[k, d - 1, b] = chip_sum(k, lax.rem(y + d, 4), b).astype(BF16)
+                start(y_copy(k, d, b))
 
     def x_copy_a(k):
         return copy(
@@ -329,16 +336,19 @@
         return copy(xt.at[k, 0], xr.at[k, 2], S_X[k] + 2, dev(xl, z, 1 - xh, y, c))
 
     def x_start(k):
-        total = chip_sum(k, y)
-        for d in (1, 3, 2):
-            y_copy(k, d).wait_recv()
-            total = total + yr[k, d - 1].astype(F32)
-        xt[k] = total.astype(BF16)
-        start(x_copy_a(k))
-
-        @pl.when(xh != xl)
-        def _():
-            x_copy_b(k).start()
+        for b in (1, 0):
+            total = chip_sum(k, y, b)
+            for d in (1, 3, 2):
+                y_copy(k, d, b).wait_recv()
+                total = total + yr[k, d - 1, b].astype(F32)
+            xt[k, b] = total.astype(BF16)
+            if b == 1:
+                start(x_copy_a(k))
+            else:
+
+                @pl.when(xh != xl)
+                def _():
+                    x_copy_b(k).start()
 
     def finish(k):
         def put(branch):
@@ -397,56 +407,73 @@
     exp_cp[1][1].wait_recv()
     start(prj_cp[0])
     rs_step(1, 0, 1)
-    for s in range(1, 4):
-        ag_step(0, s, last=s == 3)
-        rs_step(1, s, 0)
-        rs_step(1, s, 1)
-        if s == 2:
-            start(prj_cp[1])
+    ag_step(0, 1)
+    ag_step(0, 2)
+    rs_step(1, 1, 0)
+    rs_step(1, 1, 1)
+    ag_step(0, 3, last=True)
+    rs_step(1, 2, 0)
+    rs_step(1, 2, 1)
+
+    def gemm2_pair(k, s):
+        gemm2(k, lax.rem(z - s + 8, 8))
+        gemm2(k, lax.rem(z + s, 8))
+
+    project_in[0].wait()
+    project_in[1].wait()
+    prj_cp[0].wait_recv()
+    start(prj_cp[1])
+    gemm2(0, z)
+    gemm2_pair(0, 1)
+    gemm2_pair(0, 2)
+    rs_step(1, 3, 0)
+    rs_step(1, 3, 1)
+    ag_finish(0)
+    gemm2_pair(0, 3)
+    gemm2(0, lax.rem(z + 4, 8))
+    core_start(0)
     ends.append(lambda: rs_sent(1))
     ends.append(lambda: ag_sent(0))
     rs_finish(1)
 
-    def gemm2_pair(k, s):
-        gemm2(k, lax.rem(z - s + 8, 8))
-        gemm2(k, lax.rem(z + s, 8))
+    place = xh * 4 + y
+
+    def left_copy(d):
+        to = lax.rem(place + d, 8)
+        return copy(a_l, al.at[share, xh], S_LEFT + d, (i, to * 2 + c))
+
+    def left_forward(d):
+        came = lax.rem(place - d + 8, 8)
+        ref = al.at[lax.rem(came, 4) * 2 + c, lax.div(came, 4)]
+        return copy(ref, ref, S_LEFTC + d, c_peer)
+
+    def left_pass(d):
+        left_copy(d).wait_recv()
+        left_forward(d).start()
 
     ag_step(1, 0, True)
-    ag_finish(0)
-    project_in[0].wait()
-    project_in[1].wait()
-    prj_cp[0].wait_recv()
-    run(lambda r: gemm2(0, r), 0, 8)
-    start(core_copy(0))
+    y_start(0)
     ag_step(1, 1)
-    y_start(0)
     prj_cp[1].wait_recv()
     gemm2(1, z)
     gemm2_pair(1, 1)
+    x_start(0)
     ag_step(1, 2)
     gemm2_pair(1, 2)
+    finish(0)
+    al[share, xh] = a_l[...]
+    run(lambda d: left_copy(d).start(), 1, 8)
+    left_forward(0).start()
+    ends.append(lambda: run(lambda d: left_copy(d).wait_send(), 1, 8))
+    ends.append(lambda: run(lambda d: left_forward(d).wait_send(), 0, 8))
     ag_step(1, 3, last=True)
-    x_start(0)
     gemm2_pair(1, 3)
     ag_finish(1)
     ends.append(lambda: ag_sent(1))
     gemm2(1, lax.rem(z + 4, 8))
-    start(core_copy(1))
-    finish(0)
-
-    place = xh * 4 + y
+    core_start(1)
     y_start(1)
-    al[share, xh] = a_l[...]
-
-    def left_copy(d):
-        to = lax.rem(place + d, 8)
-        return copy(a_l, al.at[share, xh], S_LEFT + d, (i, to * 2 + c))
-
-    def left_forward(d):
-        came = lax.rem(place - d + 8, 8)
-        ref = al.at[lax.rem(came, 4) * 2 + c, lax.div(came, 4)]
-        return copy(ref, ref, S_LEFTC + d, c_peer)
-
+    run(left_pass, 1, 8)
     x_start(1)
     finish(1)
 
@@ -459,15 +486,6 @@
     @pl.when(i == j)
     def _():
         at[z, xl] = a_r[...]
-
-    run(lambda d: left_copy(d).start(), 1, 8)
-    left_forward(0).start()
-    ends.append(lambda: run(lambda d: left_copy(d).wait_send(), 1, 8))
-    ends.append(lambda: run(lambda d: left_forward(d).wait_send(), 0, 8))
-
-    def left_pass(d):
-        left_copy(d).wait_recv()
-        left_forward(d).start()
 
     @pl.when(i != j)
     def _():
@@ -493,12 +511,9 @@
         )
         corr[...] = term if first else corr[...] + term
 
-    def pass_right(s):
-        for which in range(2):
-            for way in range(2):
-                right_copy(s - 1, way, which).wait_recv()
-                if s < 3 or way == which:
-                    start(right_copy(s, way, which))
+    def across(n):
+        ref = at.at[lax.rem(z + (5, 3, 4)[n], 8), xl]
+        return copy(ref, ref, S_CROSS + n, x_peer)
 
     def add_pair(s):
         add(lax.rem(z - s + 8, 8))
@@ -509,18 +524,30 @@
     pair.wait_recv()
     for way in range(2):
         start(right_copy(0, way, 1))
-    run(left_pass, 1, 4)
-    pass_right(1)
-    run(left_pass, 4, 8)
-    pass_right(2)
+    for which in range(2):
+        for way in range(2):
+            right_copy(0, way, which).wait_recv()
+            start(right_copy(1, way, which))
+    for way in range(2):
+        right_copy(1, way, 0).wait_recv()
+        start(right_copy(2, way, 0))
     run(lambda d: left_forward(d).wait_recv(), 0, 8)
     add(z, True)
     add_pair(1)
-    pass_right(3)
+    right_copy(2, 0, 0).wait_recv()
+    start(right_copy(3, 0, 0))
+    start(across(0))
+    right_copy(2, 1, 0).wait_recv()
+    start(across(1))
+    for way in range(2):
+        right_copy(1, way, 1).wait_recv()
     add_pair(2)
+    right_copy(3, 0, 0).wait_recv()
+    start(across(2))
+    across(0).wait_recv()
+    across(1).wait_recv()
     add_pair(3)
-    for way in range(2):
-        right_copy(3, way, way).wait_recv()
+    across(2).wait_recv()
     add(lax.rem(z + 4, 8))
     drain()
 
@@ -559,8 +586,8 @@
             pltpu.VMEM((2, 4, 2, 2) + tile, BF16),
             pltpu.VMEM((2, 4, 2, 2) + tile, BF16),
             pltpu.VMEM((2, 8, 2) + tile, BF16),
-            pltpu.VMEM((2, 2, 4, 2) + tile, BF16),
-            pltpu.VMEM((2, 4, 2) + tile, BF16),
+            pltpu.VMEM((2, 2, 2, 4) + tile, BF16),
+            pltpu.VMEM((2, 2, 4) + tile, BF16),
             pltpu.VMEM((2, 3, 2) + tile, BF16),
             pltpu.VMEM((2, 3, 2) + tile, BF16),
             pltpu.VMEM((2, 2) + tile, BF16),

time: 162 us -> 155 us (0.957)
  the two profiles are of different devices: /device:TPU:40 before, /device:TPU:32 now
where the time goes in v4:
time: 155 us
  Pallas kernels  154 us (99%)
    pallas_call x1, Pallas kernels, per_device(): pl.pallas_call(kernel, out_shape=shapes, in_specs=[hbm, hbm, vm, vm, hbm,...  152 us

profile of v4, /device:TPU:32, one launch (start us, length us, event | category | flops | bytes accessed | tf_op | source)
XLA Modules:
  0.0 154.8 jit_solution(4454879908621576845)
XLA Ops:
  0.6 152.1 %shard_map.139 = (bf16[128,384]{1,0:T(8,128)(2,1)}, bf16[128,384]{1,0:T(8,128)(2,1)}, f32[384,384]{1,0:T(8,128)}) custom-call(bf16[2048,384]{1,0:T(8,128)(2,1)} %s_l.1, bf16[2048,384]{1,0:T(8,128)(2,1)} %s_r.1, f32[384]{0:T(512)} %g_l.1, f32[384]{0:T(512)} %g_r.1, bf16[384,768]{1,0:T(8,128)(2,1)} %e_l.1, bf16[384,768]{1,0:T(8,128)(2,1)} %e_r.1, f32[768]{0:T(1024)} %b_l.1, ...), custom_call_target="tpu_custom_call" | custom-call | tf_op jit(solution)/shard_map/pallas_call | solution.py:570
  152.7 2.1 %shard_map.140 = (bf16[128,384]{1,0:T(8,128)(2,1)}, bf16[128,384]{1,0:T(8,128)(2,1)}, f32[384,384]{1,0:T(8,128)}) custom-call(bf16[128,384]{1,0:T(8,128)(2,1)} %get-tuple-element.6.a_l, bf16[128,384]{1,0:T(8,128)(2,1)} %get-tuple-element.7.a_r, f32[384,384]{1,0:T(8,128)} %get-tuple-element.8.corr), custom_call_target="tpu_custom_call" | custom-call | tf_op jit(solution)/shard_map/pallas_call | solution.py:609

commit v5 on v4

--- a/solution.py
+++ b/solution.py
@@ -35,17 +35,17 @@
 S_PROJ = [SLOTS.take(1) for _ in range(2)]
 S_GAIN = [SLOTS.take(1) for _ in range(2)]
 S_STREAM = [SLOTS.take(16) for _ in range(2)]
-S_RS = [SLOTS.take(16) for _ in range(2)]
-S_AG = [SLOTS.take(16) for _ in range(2)]
+S_RS = [SLOTS.take(32) for _ in range(2)]
+S_AG = [SLOTS.take(32) for _ in range(2)]
 S_CORE = [SLOTS.take(2) for _ in range(2)]
 S_Y = [SLOTS.take(8) for _ in range(2)]
 S_X = [SLOTS.take(3) for _ in range(2)]
 S_LEFT = SLOTS.take(8)
 S_LEFTC = SLOTS.take(8)
-S_TURN = SLOTS.take(1)
-S_PAIR = SLOTS.take(1)
-S_RIGHT = SLOTS.take(16)
-S_CROSS = SLOTS.take(3)
+S_TURN = SLOTS.take(2)
+S_PAIR = SLOTS.take(2)
+S_RIGHT = SLOTS.take(32)
+S_CROSS = SLOTS.take(6)
 N_SEMS = SLOTS.count
 
 
@@ -241,61 +241,74 @@
         own = jnp.dot(nrm[k, r, 0], ev[k, :, cols(h)], preferred_element_type=F32)
         return own + jnp.dot(nrm[k, r, 1], xe[k, h], preferred_element_type=F32)
 
-    def rs_copy(k, s, way, half):
-        sem = S_RS[k] + 4 * s + 2 * way + half
-        return copy(rsb.at[k, s, way, half], rr.at[k, s, way, half], sem, (z_next, z_prev)[way])
+    def piece(ref, u):
+        return ref.at[pl.ds(u * 64, 64)]
+
+    def rs_copy(k, s, way, half, u):
+        sem = S_RS[k] + 8 * s + 4 * way + 2 * half + u
+        src, dst = rsb.at[k, s, way, half], rr.at[k, s, way, half]
+        return copy(piece(src, u), piece(dst, u), sem, (z_next, z_prev)[way])
 
     def rs_step(k, s, half):
-        for way in range(2):
-            if s == 0 and half != way:
-                continue
+        ways = [way for way in range(2) if s > 0 or half == way]
+        own = {}
+        for way in ways:
             r = lax.rem(z + 4 - s + 8, 8) if way == 0 else lax.rem(z + 4 + s, 8)
-            acc = partial_pre(k, r, half)
-            if s > 1 or (s == 1 and half == way):
-                rs_copy(k, s - 1, way, half).wait_recv()
-                acc = acc + rr[k, s - 1, way, half].astype(F32)
-            rsb[k, s, way, half] = acc.astype(BF16)
-            rs_copy(k, s, way, half).start()
+            own[way] = partial_pre(k, r, half)
+        for u in range(2):
+            rows = slice(u * 64, (u + 1) * 64)
+            for way in ways:
+                acc = own[way][rows]
+                if s > 1 or (s == 1 and half == way):
+                    rs_copy(k, s - 1, way, half, u).wait_recv()
+                    acc = acc + rr[k, s - 1, way, half, rows].astype(F32)
+                rsb[k, s, way, half, rows] = acc.astype(BF16)
+                rs_copy(k, s, way, half, u).start()
 
     def rs_sent(k):
-        for way in range(2):
-            rs_copy(k, 0, way, way).wait_send()
-            for half in range(2):
-                run(lambda s: rs_copy(k, s, way, half).wait_send(), 1, 4)
+        for u in range(2):
+            for way in range(2):
+                rs_copy(k, 0, way, way, u).wait_send()
+                for half in range(2):
+                    run(lambda s: rs_copy(k, s, way, half, u).wait_send(), 1, 4)
 
     def rs_finish(k):
         for half in range(2):
             acc = partial_pre(k, z, half) + shifts[k][cols(half)].reshape(1, W)
             for way in range(2):
-                rs_copy(k, 3, way, half).wait_recv()
+                for u in range(2):
+                    rs_copy(k, 3, way, half, u).wait_recv()
                 acc = acc + rr[k, 3, way, half].astype(F32)
             act[k, z, half] = (0.5 * acc * (1.0 + lax.erf(acc * (0.5 ** 0.5)))).astype(BF16)
 
-    def ag_copy(k, s, way, half):
+    def ag_copy(k, s, way, half, u):
         if way == 0:
             r, to = lax.rem(z - s + 8, 8), z_next
         else:
             r, to = lax.rem(z + s, 8), z_prev
-        ref = act.at[k, r, half]
-        return copy(ref, ref, S_AG[k] + 4 * s + 2 * way + half, to)
+        ref = piece(act.at[k, r, half], u)
+        return copy(ref, ref, S_AG[k] + 8 * s + 4 * way + 2 * half + u, to)
 
     def ag_step(k, s, first=False, last=False):
         for half in range(2):
+            for u in range(2):
+                for way in range(2):
+                    if not first:
+                        ag_copy(k, s - 1, way, half, u).wait_recv()
+                    if not last or half == way:
+                        ag_copy(k, s, way, half, u).start()
+
+    def ag_finish(k):
+        for u in range(2):
             for way in range(2):
-                if not first:
-                    ag_copy(k, s - 1, way, half).wait_recv()
-                if not last or half == way:
-                    ag_copy(k, s, way, half).start()
-
-    def ag_finish(k):
-        for way in range(2):
-            ag_copy(k, 3, way, way).wait_recv()
+                ag_copy(k, 3, way, way, u).wait_recv()
 
     def ag_sent(k):
-        for way in range(2):
-            for half in range(2):
-                run(lambda s: ag_copy(k, s, way, half).wait_send(), 0, 3)
-            ag_copy(k, 3, way, way).wait_send()
+        for u in range(2):
+            for way in range(2):
+                for half in range(2):
+                    run(lambda s: ag_copy(k, s, way, half, u).wait_send(), 0, 3)
+                ag_copy(k, 3, way, way, u).wait_send()
 
     def gemm2(k, r):
         for b, weight in enumerate((pv.at[k], xp.at[k])):
@@ -399,14 +412,14 @@
         ends.append(lambda k=k: run(lambda n: stream_forward(k, n).wait_send(), 0, 8))
     ends.append(lambda: rs_sent(0))
 
-    rs_finish(0)
-    ag_step(0, 0, True)
     expand_in[1].wait()
     exp_cp[1][0].wait_recv()
     rs_step(1, 0, 0)
     exp_cp[1][1].wait_recv()
     start(prj_cp[0])
     rs_step(1, 0, 1)
+    rs_finish(0)
+    ag_step(0, 0, True)
     ag_step(0, 1)
     ag_step(0, 2)
     rs_step(1, 1, 0)
@@ -457,17 +470,17 @@
     prj_cp[1].wait_recv()
     gemm2(1, z)
     gemm2_pair(1, 1)
-    x_start(0)
     ag_step(1, 2)
     gemm2_pair(1, 2)
+    x_start(0)
+    ag_step(1, 3, last=True)
+    gemm2_pair(1, 3)
     finish(0)
     al[share, xh] = a_l[...]
     run(lambda d: left_copy(d).start(), 1, 8)
     left_forward(0).start()
     ends.append(lambda: run(lambda d: left_copy(d).wait_send(), 1, 8))
     ends.append(lambda: run(lambda d: left_forward(d).wait_send(), 0, 8))
-    ag_step(1, 3, last=True)
-    gemm2_pair(1, 3)
     ag_finish(1)
     ends.append(lambda: ag_sent(1))
     gemm2(1, lax.rem(z + 4, 8))
@@ -477,30 +490,30 @@
     x_start(1)
     finish(1)
 
-    turn = copy(a_r, at.at[lax.rem(j, 8), lax.div(j, 8)], S_TURN, (j, i))
+    def turn(u):
+        there = piece(at.at[lax.rem(j, 8), lax.div(j, 8)], u)
+        return copy(piece(a_r, u), there, S_TURN + u, (j, i))
 
     @pl.when(i != j)
     def _():
-        turn.start()
+        turn(0).start()
+        turn(1).start()
 
     @pl.when(i == j)
     def _():
         at[z, xl] = a_r[...]
 
-    @pl.when(i != j)
-    def _():
-        turn.wait()
-
-    here = at.at[z, xl]
-    pair = start(copy(here, here, S_PAIR, x_peer))
-
-    def right_copy(s, way, which):
+    def pair(u):
+        here = piece(at.at[z, xl], u)
+        return copy(here, here, S_PAIR + u, x_peer)
+
+    def right_copy(s, way, which, u):
         if way == 0:
             r, to = lax.rem(z - s + 8, 8), z_next
         else:
             r, to = lax.rem(z + s, 8), z_prev
-        ref = at.at[r, xl if which == 0 else 1 - xl]
-        return copy(ref, ref, S_RIGHT + 4 * s + 2 * way + which, to)
+        ref = piece(at.at[r, xl if which == 0 else 1 - xl], u)
+        return copy(ref, ref, S_RIGHT + 8 * s + 4 * way + 2 * which + u, to)
 
     def add(r, first=False):
         term = lax.dot_general(
@@ -511,44 +524,61 @@
         )
         corr[...] = term if first else corr[...] + term
 
-    def across(n):
-        ref = at.at[lax.rem(z + (5, 3, 4)[n], 8), xl]
-        return copy(ref, ref, S_CROSS + n, x_peer)
+    def across(n, u):
+        ref = piece(at.at[lax.rem(z + (5, 3, 4)[n], 8), xl], u)
+        return copy(ref, ref, S_CROSS + 2 * n + u, x_peer)
 
     def add_pair(s):
         add(lax.rem(z - s + 8, 8))
         add(lax.rem(z + s, 8))
 
-    for way in range(2):
-        start(right_copy(0, way, 0))
-    pair.wait_recv()
-    for way in range(2):
-        start(right_copy(0, way, 1))
-    for which in range(2):
+    for u in range(2):
+
+        @pl.when(i != j)
+        def _(u=u):
+            turn(u).wait_recv()
+
         for way in range(2):
-            right_copy(0, way, which).wait_recv()
-            start(right_copy(1, way, which))
-    for way in range(2):
-        right_copy(1, way, 0).wait_recv()
-        start(right_copy(2, way, 0))
+            start(right_copy(0, way, 0, u))
+        start(pair(u))
+    for u in range(2):
+        pair(u).wait_recv()
+        for way in range(2):
+            start(right_copy(0, way, 1, u))
+    for s, which in ((1, 0), (1, 1), (2, 0)):
+        for u in range(2):
+            for way in range(2):
+                right_copy(s - 1, way, which, u).wait_recv()
+                start(right_copy(s, way, which, u))
     run(lambda d: left_forward(d).wait_recv(), 0, 8)
     add(z, True)
     add_pair(1)
-    right_copy(2, 0, 0).wait_recv()
-    start(right_copy(3, 0, 0))
-    start(across(0))
-    right_copy(2, 1, 0).wait_recv()
-    start(across(1))
-    for way in range(2):
-        right_copy(1, way, 1).wait_recv()
+    for u in range(2):
+        right_copy(2, 0, 0, u).wait_recv()
+        start(right_copy(3, 0, 0, u))
+        start(across(0, u))
+        right_copy(2, 1, 0, u).wait_recv()
+        start(across(1, u))
+    for u in range(2):
+        for way in range(2):
+            right_copy(1, way, 1, u).wait_recv()
     add_pair(2)
-    right_copy(3, 0, 0).wait_recv()
-    start(across(2))
-    across(0).wait_recv()
-    across(1).wait_recv()
+    for u in range(2):
+        right_copy(3, 0, 0, u).wait_recv()
+        start(across(2, u))
+    for n in range(2):
+        for u in range(2):
+            across(n, u).wait_recv()
     add_pair(3)
-    across(2).wait_recv()
+    for u in range(2):
+        across(2, u).wait_recv()
     add(lax.rem(z + 4, 8))
+
+    @pl.when(i != j)
+    def _():
+        turn(0).wait_send()
+        turn(1).wait_send()
+
     drain()
 
 

time: 155 us -> 152 us (0.981)
  Pallas kernels: 154 us -> 150 us
    pallas_call x1, Pallas kernels: 152 us -> 148 us  [per_device(): pl.pallas_call(kernel, out_shape=shapes, in_specs=[hbm, hbm, vm, vm, hbm,...]
where the time goes in v5:
time: 152 us; the launch traced here: 151 us
  Pallas kernels  150 us (99%)
    pallas_call x1, Pallas kernels, per_device(): pl.pallas_call(kernel, out_shape=shapes, in_specs=[hbm, hbm, vm, vm, hbm,...  148 us

profile of v5, /device:TPU:32, one launch (start us, length us, event | category | flops | bytes accessed | tf_op | source)
XLA Modules:
  0.0 151.1 jit_solution(6466648636552438398)
XLA Ops:
  0.6 148.4 %shard_map.139 = (bf16[128,384]{1,0:T(8,128)(2,1)}, bf16[128,384]{1,0:T(8,128)(2,1)}, f32[384,384]{1,0:T(8,128)}) custom-call(bf16[2048,384]{1,0:T(8,128)(2,1)} %s_l.1, bf16[2048,384]{1,0:T(8,128)(2,1)} %s_r.1, f32[384]{0:T(512)} %g_l.1, f32[384]{0:T(512)} %g_r.1, bf16[384,768]{1,0:T(8,128)(2,1)} %e_l.1, bf16[384,768]{1,0:T(8,128)(2,1)} %e_r.1, f32[768]{0:T(1024)} %b_l.1, ...), custom_call_target="tpu_custom_call" | custom-call | tf_op jit(solution)/shard_map/pallas_call | solution.py:600
  149.0 2.1 %shard_map.140 = (bf16[128,384]{1,0:T(8,128)(2,1)}, bf16[128,384]{1,0:T(8,128)(2,1)}, f32[384,384]{1,0:T(8,128)}) custom-call(bf16[128,384]{1,0:T(8,128)(2,1)} %get-tuple-element.6.a_l, bf16[128,384]{1,0:T(8,128)(2,1)} %get-tuple-element.7.a_r, f32[384,384]{1,0:T(8,128)} %get-tuple-element.8.corr), custom_call_target="tpu_custom_call" | custom-call | tf_op jit(solution)/shard_map/pallas_call | solution.py:639

commit v6 on v5

--- a/solution.py
+++ b/solution.py
@@ -420,13 +420,16 @@
     rs_step(1, 0, 1)
     rs_finish(0)
     ag_step(0, 0, True)
-    ag_step(0, 1)
-    ag_step(0, 2)
-    rs_step(1, 1, 0)
-    rs_step(1, 1, 1)
-    ag_step(0, 3, last=True)
-    rs_step(1, 2, 0)
-    rs_step(1, 2, 1)
+    for s in range(1, 4):
+        rs_step(1, s, 0)
+        rs_step(1, s, 1)
+        ag_step(0, s, last=s == 3)
+        if s == 2:
+            start(prj_cp[1])
+    rs_finish(1)
+    ag_step(1, 0, True)
+    ends.append(lambda: rs_sent(1))
+    ends.append(lambda: ag_sent(0))
 
     def gemm2_pair(k, s):
         gemm2(k, lax.rem(z - s + 8, 8))
@@ -435,19 +438,13 @@
     project_in[0].wait()
     project_in[1].wait()
     prj_cp[0].wait_recv()
-    start(prj_cp[1])
     gemm2(0, z)
     gemm2_pair(0, 1)
     gemm2_pair(0, 2)
-    rs_step(1, 3, 0)
-    rs_step(1, 3, 1)
     ag_finish(0)
     gemm2_pair(0, 3)
     gemm2(0, lax.rem(z + 4, 8))
     core_start(0)
-    ends.append(lambda: rs_sent(1))
-    ends.append(lambda: ag_sent(0))
-    rs_finish(1)
 
     place = xh * 4 + y
 
@@ -464,17 +461,16 @@
         left_copy(d).wait_recv()
         left_forward(d).start()
 
-    ag_step(1, 0, True)
+    ag_step(1, 1)
     y_start(0)
-    ag_step(1, 1)
     prj_cp[1].wait_recv()
     gemm2(1, z)
     gemm2_pair(1, 1)
     ag_step(1, 2)
     gemm2_pair(1, 2)
-    x_start(0)
     ag_step(1, 3, last=True)
     gemm2_pair(1, 3)
+    x_start(0)
     finish(0)
     al[share, xh] = a_l[...]
     run(lambda d: left_copy(d).start(), 1, 8)

time: 152 us -> 154 us (1.013)
  Pallas kernels: 150 us -> 152 us
    pallas_call x1, Pallas kernels: 148 us -> 150 us  [per_device(): pl.pallas_call(kernel, out_shape=shapes, in_specs=[hbm, hbm, vm, vm, hbm,...]
where the time goes in v6:
time: 154 us; the launch traced here: 153 us
  Pallas kernels  152 us (99%)
    pallas_call x1, Pallas kernels, per_device(): pl.pallas_call(kernel, out_shape=shapes, in_specs=[hbm, hbm, vm, vm, hbm,...  150 us

profile of v6, /device:TPU:32, one launch (start us, length us, event | category | flops | bytes accessed | tf_op | source)
XLA Modules:
  0.0 153.0 jit_solution(15240387789655145847)
XLA Ops:
  0.6 150.3 %shard_map.139 = (bf16[128,384]{1,0:T(8,128)(2,1)}, bf16[128,384]{1,0:T(8,128)(2,1)}, f32[384,384]{1,0:T(8,128)}) custom-call(bf16[2048,384]{1,0:T(8,128)(2,1)} %s_l.1, bf16[2048,384]{1,0:T(8,128)(2,1)} %s_r.1, f32[384]{0:T(512)} %g_l.1, f32[384]{0:T(512)} %g_r.1, bf16[384,768]{1,0:T(8,128)(2,1)} %e_l.1, bf16[384,768]{1,0:T(8,128)(2,1)} %e_r.1, f32[768]{0:T(1024)} %b_l.1, ...), custom_call_target="tpu_custom_call" | custom-call | tf_op jit(solution)/shard_map/pallas_call | solution.py:596
  150.9 2.1 %shard_map.140 = (bf16[128,384]{1,0:T(8,128)(2,1)}, bf16[128,384]{1,0:T(8,128)(2,1)}, f32[384,384]{1,0:T(8,128)}) custom-call(bf16[128,384]{1,0:T(8,128)(2,1)} %get-tuple-element.6.a_l, bf16[128,384]{1,0:T(8,128)(2,1)} %get-tuple-element.7.a_r, f32[384,384]{1,0:T(8,128)} %get-tuple-element.8.corr), custom_call_target="tpu_custom_call" | custom-call | tf_op jit(solution)/shard_map/pallas_call | solution.py:635

commit v7 on v5

--- a/solution.py
+++ b/solution.py
@@ -42,6 +42,7 @@
 S_X = [SLOTS.take(3) for _ in range(2)]
 S_LEFT = SLOTS.take(8)
 S_LEFTC = SLOTS.take(8)
+S_LEFTX = SLOTS.take(1)
 S_TURN = SLOTS.take(2)
 S_PAIR = SLOTS.take(2)
 S_RIGHT = SLOTS.take(32)
@@ -449,20 +450,25 @@
     ends.append(lambda: ag_sent(0))
     rs_finish(1)
 
-    place = xh * 4 + y
-
-    def left_copy(d):
-        to = lax.rem(place + d, 8)
-        return copy(a_l, al.at[share, xh], S_LEFT + d, (i, to * 2 + c))
-
-    def left_forward(d):
-        came = lax.rem(place - d + 8, 8)
-        ref = al.at[lax.rem(came, 4) * 2 + c, lax.div(came, 4)]
-        return copy(ref, ref, S_LEFTC + d, c_peer)
-
-    def left_pass(d):
-        left_copy(d).wait_recv()
-        left_forward(d).start()
+    def tile_of(far, back):
+        row = lax.rem(y - back + 4, 4)
+        return al.at[row * 2 + c, xh + far * (1 - 2 * xh)]
+
+    def left_y(far, d):
+        ref = tile_of(far, 0)
+        return copy(ref, ref, S_LEFT + 4 * far + d, dev(xl, z, xh, lax.rem(y + d, 4), c))
+
+    def left_x():
+        ref = tile_of(0, 0)
+        return copy(ref, ref, S_LEFTX, dev(xl, z, 1 - xh, y, c))
+
+    def left_forward(n):
+        ref = tile_of(lax.div(n, 4), lax.rem(n, 4))
+        return copy(ref, ref, S_LEFTC + n, c_peer)
+
+    def left_pass(far, d):
+        left_y(far, d).wait_recv()
+        left_forward(4 * far + d).start()
 
     ag_step(1, 0, True)
     y_start(0)
@@ -477,16 +483,21 @@
     gemm2_pair(1, 3)
     finish(0)
     al[share, xh] = a_l[...]
-    run(lambda d: left_copy(d).start(), 1, 8)
+    start(left_x())
+    for d in (2, 1, 3):
+        start(left_y(0, d))
     left_forward(0).start()
-    ends.append(lambda: run(lambda d: left_copy(d).wait_send(), 1, 8))
-    ends.append(lambda: run(lambda d: left_forward(d).wait_send(), 0, 8))
+    ends.append(lambda: run(lambda n: left_forward(n).wait_send(), 0, 8))
     ag_finish(1)
     ends.append(lambda: ag_sent(1))
     gemm2(1, lax.rem(z + 4, 8))
     core_start(1)
     y_start(1)
-    run(left_pass, 1, 8)
+    left_x().wait_recv()
+    for d in (2, 1, 3):
+        start(left_y(1, d))
+    left_forward(4).start()
+    run(lambda d: left_pass(0, d), 1, 4)
     x_start(1)
     finish(1)
 
@@ -550,7 +561,8 @@
             for way in range(2):
                 right_copy(s - 1, way, which, u).wait_recv()
                 start(right_copy(s, way, which, u))
-    run(lambda d: left_forward(d).wait_recv(), 0, 8)
+    run(lambda d: left_pass(1, d), 1, 4)
+    run(lambda n: left_forward(n).wait_recv(), 0, 8)
     add(z, True)
     add_pair(1)
     for u in range(2):

time: 152 us -> 152 us (level); the launches traced: 151 us -> 149 us
  Pallas kernels: 150 us -> 148 us
    pallas_call x1, Pallas kernels: 148 us -> 146 us  [per_device(): pl.pallas_call(kernel, out_shape=shapes, in_specs=[hbm, hbm, vm, vm, hbm,...]
where the time goes in v7:
time: 152 us; the launch traced here: 149 us
  Pallas kernels  148 us (97%)
    pallas_call x1, Pallas kernels, per_device(): pl.pallas_call(kernel, out_shape=shapes, in_specs=[hbm, hbm, vm, vm, hbm,...  146 us

profile of v7, /device:TPU:32, one launch (start us, length us, event | category | flops | bytes accessed | tf_op | source)
XLA Modules:
  0.0 148.8 jit_solution(5455391629508208029)
XLA Ops:
  0.6 146.1 %shard_map.139 = (bf16[128,384]{1,0:T(8,128)(2,1)}, bf16[128,384]{1,0:T(8,128)(2,1)}, f32[384,384]{1,0:T(8,128)}) custom-call(bf16[2048,384]{1,0:T(8,128)(2,1)} %s_l.1, bf16[2048,384]{1,0:T(8,128)(2,1)} %s_r.1, f32[384]{0:T(512)} %g_l.1, f32[384]{0:T(512)} %g_r.1, bf16[384,768]{1,0:T(8,128)(2,1)} %e_l.1, bf16[384,768]{1,0:T(8,128)(2,1)} %e_r.1, f32[768]{0:T(1024)} %b_l.1, ...), custom_call_target="tpu_custom_call" | custom-call | tf_op jit(solution)/shard_map/pallas_call | solution.py:612
  146.7 2.1 %shard_map.140 = (bf16[128,384]{1,0:T(8,128)(2,1)}, bf16[128,384]{1,0:T(8,128)(2,1)}, f32[384,384]{1,0:T(8,128)}) custom-call(bf16[128,384]{1,0:T(8,128)(2,1)} %get-tuple-element.6.a_l, bf16[128,384]{1,0:T(8,128)(2,1)} %get-tuple-element.7.a_r, f32[384,384]{1,0:T(8,128)} %get-tuple-element.8.corr), custom_call_target="tpu_custom_call" | custom-call | tf_op jit(solution)/shard_map/pallas_call | solution.py:651

commit v8 on v7

--- a/solution.py
+++ b/solution.py
@@ -421,13 +421,16 @@
     rs_step(1, 0, 1)
     rs_finish(0)
     ag_step(0, 0, True)
-    ag_step(0, 1)
-    ag_step(0, 2)
-    rs_step(1, 1, 0)
-    rs_step(1, 1, 1)
-    ag_step(0, 3, last=True)
-    rs_step(1, 2, 0)
-    rs_step(1, 2, 1)
+    for s in range(1, 4):
+        rs_step(1, s, 0)
+        rs_step(1, s, 1)
+        ag_step(0, s, last=s == 3)
+        if s == 2:
+            start(prj_cp[1])
+    rs_finish(1)
+    ag_step(1, 0, True)
+    ends.append(lambda: rs_sent(1))
+    ends.append(lambda: ag_sent(0))
 
     def gemm2_pair(k, s):
         gemm2(k, lax.rem(z - s + 8, 8))
@@ -436,19 +439,13 @@
     project_in[0].wait()
     project_in[1].wait()
     prj_cp[0].wait_recv()
-    start(prj_cp[1])
     gemm2(0, z)
     gemm2_pair(0, 1)
     gemm2_pair(0, 2)
-    rs_step(1, 3, 0)
-    rs_step(1, 3, 1)
     ag_finish(0)
     gemm2_pair(0, 3)
     gemm2(0, lax.rem(z + 4, 8))
     core_start(0)
-    ends.append(lambda: rs_sent(1))
-    ends.append(lambda: ag_sent(0))
-    rs_finish(1)
 
     def tile_of(far, back):
         row = lax.rem(y - back + 4, 4)
@@ -470,35 +467,34 @@
         left_y(far, d).wait_recv()
         left_forward(4 * far + d).start()
 
-    ag_step(1, 0, True)
+    ag_step(1, 1)
     y_start(0)
-    ag_step(1, 1)
     prj_cp[1].wait_recv()
     gemm2(1, z)
     gemm2_pair(1, 1)
     ag_step(1, 2)
     gemm2_pair(1, 2)
-    x_start(0)
     ag_step(1, 3, last=True)
     gemm2_pair(1, 3)
+    x_start(0)
+    ag_finish(1)
+    ends.append(lambda: ag_sent(1))
+    gemm2(1, lax.rem(z + 4, 8))
+    core_start(1)
     finish(0)
+    y_start(1)
     al[share, xh] = a_l[...]
     start(left_x())
     for d in (2, 1, 3):
         start(left_y(0, d))
     left_forward(0).start()
     ends.append(lambda: run(lambda n: left_forward(n).wait_send(), 0, 8))
-    ag_finish(1)
-    ends.append(lambda: ag_sent(1))
-    gemm2(1, lax.rem(z + 4, 8))
-    core_start(1)
-    y_start(1)
     left_x().wait_recv()
     for d in (2, 1, 3):
         start(left_y(1, d))
     left_forward(4).start()
+    x_start(1)
     run(lambda d: left_pass(0, d), 1, 4)
-    x_start(1)
     finish(1)
 
     def turn(u):

time: 152 us -> 148 us (0.974); the launches traced: 149 us -> 147 us
  Pallas kernels: 148 us -> 146 us
    pallas_call x1, Pallas kernels: 146 us -> 144 us  [per_device(): pl.pallas_call(kernel, out_shape=shapes, in_specs=[hbm, hbm, vm, vm, hbm,...]
where the time goes in v8:
time: 148 us; the launch traced here: 147 us
  Pallas kernels  146 us (99%)
    pallas_call x1, Pallas kernels, per_device(): pl.pallas_call(kernel, out_shape=shapes, in_specs=[hbm, hbm, vm, vm, hbm,...  144 us

profile of v8, /device:TPU:32, one launch (start us, length us, event | category | flops | bytes accessed | tf_op | source)
XLA Modules:
  0.0 147.0 jit_solution(16029852619569296588)
XLA Ops:
  0.6 144.3 %shard_map.139 = (bf16[128,384]{1,0:T(8,128)(2,1)}, bf16[128,384]{1,0:T(8,128)(2,1)}, f32[384,384]{1,0:T(8,128)}) custom-call(bf16[2048,384]{1,0:T(8,128)(2,1)} %s_l.1, bf16[2048,384]{1,0:T(8,128)(2,1)} %s_r.1, f32[384]{0:T(512)} %g_l.1, f32[384]{0:T(512)} %g_r.1, bf16[384,768]{1,0:T(8,128)(2,1)} %e_l.1, bf16[384,768]{1,0:T(8,128)(2,1)} %e_r.1, f32[768]{0:T(1024)} %b_l.1, ...), custom_call_target="tpu_custom_call" | custom-call | tf_op jit(solution)/shard_map/pallas_call | solution.py:608
  144.9 2.1 %shard_map.140 = (bf16[128,384]{1,0:T(8,128)(2,1)}, bf16[128,384]{1,0:T(8,128)(2,1)}, f32[384,384]{1,0:T(8,128)}) custom-call(bf16[128,384]{1,0:T(8,128)(2,1)} %get-tuple-element.6.a_l, bf16[128,384]{1,0:T(8,128)(2,1)} %get-tuple-element.7.a_r, f32[384,384]{1,0:T(8,128)} %get-tuple-element.8.corr), custom_call_target="tpu_custom_call" | custom-call | tf_op jit(solution)/shard_map/pallas_call | solution.py:647
